TPU v7x, 256 devices: a whole 4x4x8 slice. The times are simulated.
256 devices in a mesh: dp: 8 (over z), seq: 32 (over y, x, core).
Axes of the slice: x: 4, y: 4, z: 8, core: 2. Of those that a mesh axis runs over, the one named last changes fastest.
Arguments:
- embeddings: bfloat16 [8, 4096, 1536], P('dp', 'seq'), may hold values from -6 to 6
- conv_one: bfloat16 [3, 1536, 1536], P(None, 'dp'), may hold values from -0.09375 to 0.09375
- conv_two: bfloat16 [3, 1536, 1536], P(None, 'dp'), may hold values from -0.09375 to 0.09375
- head_weight: bfloat16 [1536, 3072], P(None, 'dp'), may hold values from -4 to 4
- counts: int32 [8, 4096, 3072], P(None, 'seq', 'dp'), may hold values from 0 to 12
- dilation: int32 [2], replicated, may hold values from 1 to 32, as said below
Outputs:
- track_loss: float32 [8, 3072], P(None, 'dp')
- grad_head: float32 [1536, 3072], P('seq', 'dp')
- grad_one: float32 [3, 1536, 1536], P(None, 'seq', 'dp')
- grad_two: float32 [3, 1536, 1536], P(None, 'seq', 'dp')
Inputs may be any that keep to these rules, and one draw needn't show every extreme that they name: One of the two convolutions has dilation 32, the other a smaller one.
All inputs are finite; a program needn't handle non-finite values.
Results may differ from a plain program's by a relative error of at most 0.019.
The roundings to bfloat16 on the way count: a program that leaves them out, or rounds other values in their place, can miss the bound.
Values may be sent and summed in bfloat16 or wider, within the bound.
A program may use at most 128 MiB of HBM per device.

v0:
```python
import jax
import jax.numpy as jnp
from jax import lax
from jax.sharding import PartitionSpec as P

DMAX = 32


def with_halo(value, sides, width):
    for axis, dim in sides:
        size, length = (lax.axis_size(axis), value.shape[dim])
        up = [(i, (i + 1) % size) for i in range(size - 1)]
        down = [(j, i) for i, j in up]
        last = lax.slice_in_dim(value, length - width, length, axis=dim)
        first = lax.slice_in_dim(value, 0, width, axis=dim)
        before = lax.ppermute(last, axis, up)
        after = lax.ppermute(first, axis, down)
        value = jnp.concatenate([before, value, after], axis=dim)
    return value


def activate(value):
    return jax.nn.gelu(value)


def framed_input(block):
    gathered = lax.all_gather(block, "dp", axis=0, tiled=True)
    framed = with_halo(gathered, (("seq", 1),), DMAX)
    return framed


def framed_hidden(block):
    gathered = lax.all_gather(block, "dp", axis=2, tiled=True)
    framed = with_halo(gathered, (("seq", 1),), DMAX)
    return framed


def shifted_taps(padded, spacing, length, sign):
    return [
        lax.dynamic_slice_in_dim(padded, DMAX + sign * (tap_index - 1) * spacing, length, 1)
        for tap_index in range(3)
    ]


def conv_apply(padded, weight, spacing, length):
    tap_list = shifted_taps(padded, spacing, length, 1)
    running = jnp.einsum("blc,dc->bld", tap_list[0], weight[0], preferred_element_type=jnp.float32)
    for tap_index in (1, 2):
        running = running + jnp.einsum(
            "blc,dc->bld",
            tap_list[tap_index],
            weight[tap_index],
            preferred_element_type=jnp.float32,
        )
    return running


def weight_grad(padded, upstream, spacing, length):
    tap_list = shifted_taps(padded, spacing, length, 1)
    stacked = jnp.stack(
        [
            jnp.einsum("blc,bld->cd", tap_rows, upstream, preferred_element_type=jnp.float32)
            for tap_rows in tap_list
        ]
    )
    return lax.psum_scatter(stacked, "seq", scatter_dimension=1, tiled=True)


def on_device(embeddings, conv_one, conv_two, head_weight, counts, dilation):
    length = embeddings.shape[1]
    chan_dev = conv_one.shape[1]
    own_index = lax.axis_index("dp")
    first_gap = dilation[0]
    second_gap = dilation[1]
    framed_in = framed_input(embeddings)
    pre_one = conv_apply(framed_in, conv_one, first_gap, length)
    centre_in = lax.dynamic_slice_in_dim(framed_in, DMAX, length, 1)
    own_in = lax.dynamic_slice_in_dim(centre_in, own_index * chan_dev, chan_dev, 2)
    hidden_one = (own_in.astype(jnp.float32) + activate(pre_one)).astype(jnp.bfloat16)
    framed_one = framed_hidden(hidden_one)
    pre_two = conv_apply(framed_one, conv_two, second_gap, length)
    hidden_two = (hidden_one.astype(jnp.float32) + activate(pre_two)).astype(jnp.bfloat16)
    head_rows = lax.all_gather(hidden_two, "dp", axis=2, tiled=True)
    logits = jnp.einsum("blc,ct->blt", head_rows, head_weight, preferred_element_type=jnp.float32)
    targets = counts.astype(jnp.float32)
    local_peak = jnp.max(logits, axis=1)
    count_local = jnp.sum(targets, axis=1)
    cross_local = jnp.sum(targets * logits, axis=1)
    peak_all = lax.pmax(local_peak, "seq")
    exp_local = jnp.sum(jnp.exp(logits - peak_all[:, None, :]), axis=1)
    exp_total, count_total, cross_total = lax.psum((exp_local, count_local, cross_local), "seq")
    all_bins = length * lax.axis_size("seq")
    log_total = peak_all + jnp.log(exp_total)
    track_loss = (count_total * log_total - cross_total) / all_bins
    logit_grad = (
        (count_total[:, None, :] * jnp.exp(logits - log_total[:, None, :]) - targets) / all_bins
    ).astype(jnp.bfloat16)
    grad_head = lax.psum_scatter(
        jnp.einsum("blc,blt->ct", head_rows, logit_grad, preferred_element_type=jnp.float32),
        "seq",
        scatter_dimension=0,
        tiled=True,
    )
    back_partial = jnp.einsum(
        "blt,ct->blc", logit_grad, head_weight, preferred_element_type=jnp.float32
    )
    grad_two_out = lax.psum_scatter(
        back_partial.astype(jnp.bfloat16), "dp", scatter_dimension=2, tiled=True
    ).astype(jnp.float32)
    upstream_two = jax.vjp(activate, pre_two)[1](grad_two_out)[0].astype(jnp.bfloat16)
    grad_two = weight_grad(framed_one, upstream_two, second_gap, length)
    framed_back = with_halo(upstream_two, (("seq", 1),), DMAX)
    back_taps = shifted_taps(framed_back, second_gap, length, -1)
    conv_partial = jnp.einsum(
        "bld,dc->blc", back_taps[0], conv_two[0], preferred_element_type=jnp.float32
    )
    for tap_index in (1, 2):
        conv_partial = conv_partial + jnp.einsum(
            "bld,dc->blc",
            back_taps[tap_index],
            conv_two[tap_index],
            preferred_element_type=jnp.float32,
        )
    grad_one_out = grad_two_out + lax.psum_scatter(
        conv_partial.astype(jnp.bfloat16), "dp", scatter_dimension=2, tiled=True
    ).astype(jnp.float32)
    upstream_one = jax.vjp(activate, pre_one)[1](grad_one_out)[0].astype(jnp.bfloat16)
    grad_one = weight_grad(framed_in, upstream_one, first_gap, length)
    return (track_loss, grad_head, grad_one, grad_two)


def solution(mesh):
    placed = (
        P("dp", "seq", None),
        P(None, "dp", None),
        P(None, "dp", None),
        P(None, "dp"),
        P(None, "seq", "dp"),
        P(),
    )
    return jax.shard_map(
        on_device,
        mesh=mesh,
        in_specs=placed,
        out_specs=(P(None, "dp"), P("seq", "dp"), P(None, "seq", "dp"), P(None, "seq", "dp")),
        check_vma=False,
    )
```

profile of v0, /device:TPU:2, one launch (start us, length us, event | category | flops | bytes accessed | tf_op | source)
XLA Modules:
  0.0 855.1 jit_solution(11263345450934468903)
XLA Ops:
  8.0 49.8 %all-gather.4.cloned.1.call-done = bf16[8,128,1536]{2,1,0:T(8,128)(2,1)} async-done(((bf16[1,128,1536]{2,1,0:T(8,128)(2,1)}), bf16[8,128,1536]{2,1,0:T(8,128)(2,1)}) %all-gather.4.cloned.1.call-update) | async-done | bytes 3145744 | tf_op jit(solution)/shard_map/all_gather | solution.py:27
  57.8 2.4 fusion.100
  60.2 1.9 collective-permute-start
  64.6 1.4 constant_dynamic-slice_fusion
  67.0 3.9 collective-permute-start.1
  70.9 3.2 fusion.75
  74.4 6.0 collective-permute-done.1
  80.4 1.2 fusion.13
  81.7 2.4 add_convert_fusion.2
  85.1 46.6 %all-gather.6.cloned.1.call-done = bf16[8,128,1536]{1,0,2:T(8,128)(2,1)} async-done(((bf16[8,128,192]{1,0,2:T(8,128)(2,1)}), bf16[8,128,1536]{1,0,2:T(8,128)(2,1)}) %all-gather.6.cloned.1.call-update) | async-done | bytes 3145744 | tf_op jit(solution)/shard_map/all_gather | solution.py:33
  131.7 5.0 copy.37
  136.8 2.8 fusion.99
  139.5 1.9 collective-permute-start.2
  141.5 3.6 collective-permute-start.3
  147.1 3.2 fusion.69
  150.3 2.9 collective-permute-done.2
  153.2 1.8 collective-permute-done.3
  154.9 1.6 pad_maximum_fusion
  157.7 2.4 add_convert_fusion.1
  161.2 46.6 %all-gather.8.cloned.1.call-done = bf16[8,128,1536]{1,0,2:T(8,128)(2,1)} async-done(((bf16[8,128,192]{1,0,2:T(8,128)(2,1)}), bf16[8,128,1536]{1,0,2:T(8,128)(2,1)}) %all-gather.8.cloned.1.call-update) | async-done | bytes 3145744 | tf_op jit(solution)/shard_map/all_gather | solution.py:83
  207.8 4.9 fusion.103
  212.8 122.4 %pmax.7 = f32[8,384]{1,0:T(8,128)S(1)} all-reduce(f32[8,384]{1,0:T(8,128)S(1)} %get-tuple-element.34), channel_id=1, replica_groups=mesh['dp'=8,'seq'=32] {'seq'}, use_global_device_ids=true, to_apply=%region_3.0 | all-reduce | flops 3072 | bytes 24576 | tf_op jit(solution)/shard_map/pmax | solution.py:89
  335.2 1.9 exponential_reduce_fusion
  337.1 124.0 %all-reduce.2 = (f32[8,384]{1,0:T(8,128)S(1)}, f32[8,384]{1,0:T(8,128)S(1)}, f32[8,384]{1,0:T(8,128)S(1)}) all-reduce(f32[8,384]{1,0:T(8,128)S(1)} %get-tuple-element.13, f32[8,384]{1,0:T(8,128)S(1)} %get-tuple-element.14, f32[8,384]{1,0:T(8,128)S(1)} %get-tuple-element.12), channel_id=1, replica_groups=mesh['dp'=8,'seq'=32] {'seq'}, use_global_device_ids=true, to_apply=%region_7.0 | all-reduce | flops 9216 | bytes 73728 | tf_op jit(solution)/shard_map/psum | solution.py:91
  461.7 1.8 multiply_convert_fusion
  463.6 2.1 convolution_convert_fusion
  465.6 10.1 %copy.44 = bf16[8,128,1536]{1,0,2:T(8,128)(2,1)} copy(bf16[8,128,1536]{1,2,0:T(8,128)(2,1)S(1)} %convolution_convert_fusion) | data formatting | bytes 6291456 | tf_op jit(solution)/shard_map/convert_element_type | solution.py:108
  475.8 46.3 %reduce-scatter.6.cloned.1.call-done = bf16[8,128,192]{1,0,2:T(8,128)(2,1)} async-done(((bf16[8,128,1536]{1,0,2:T(8,128)(2,1)}), bf16[8,128,192]{1,0,2:T(8,128)(2,1)}) %reduce-scatter.6.cloned.1.call-update) | async-done | bytes 393232 | tf_op jit(solution)/shard_map/reduce_scatter | solution.py:107
  522.1 1.6 fusion.58
  523.8 1.9 collective-permute-start.4
  525.8 3.9 collective-permute-start.5
  530.7 2.2 collective-permute-done.4
  532.9 1.8 collective-permute-done.5
  536.3 1.4 add_convert_fusion
  537.7 10.1 %copy.46 = bf16[8,128,1536]{1,0,2:T(8,128)(2,1)} copy(bf16[8,128,1536]{1,2,0:T(8,128)(2,1)S(1)} %add_convert_fusion) | data formatting | bytes 6291456 | tf_op jit(solution)/shard_map/convert_element_type | solution.py:125
  548.2 2.9 fusion.28
  551.1 3.2 fusion.25
  555.1 2.1 pad_maximum_fusion.2
  557.2 6.8 copy.50
  564.0 33.3 %reduce-scatter.8.cloned.1.call-done = bf16[8,128,192]{1,0,2:T(8,128)(2,1)} async-done(((bf16[8,128,1536]{1,0,2:T(8,128)(2,1)}), bf16[8,128,192]{1,0,2:T(8,128)(2,1)}) %reduce-scatter.8.cloned.1.call-update) | async-done | bytes 393232 | tf_op jit(solution)/shard_map/reduce_scatter | solution.py:124
  597.3 1.6 fusion.51
  598.9 3.0 fusion.19
  601.9 3.2 fusion.22
  605.9 2.0 pad_maximum_fusion.1
  607.8 6.7 copy.48
  615.7 5.2 convolution_bitcast_fusion
  622.2 135.1 %all-reduce.6.cloned.1.call-done = (f32[3,1536,192]{2,0,1:T(4,128)}, f32[3,1536,192]{2,0,1:T(4,128)}) async-done(((f32[3,1536,192]{2,0,1:T(4,128)}, f32[3,1536,192]{2,0,1:T(4,128)}), (f32[3,1536,192]{2,0,1:T(4,128)}, f32[3,1536,192]{2,0,1:T(4,128)})) %all-reduce.6.cloned.1.call-update) | async-done | bytes 7077904
  759.8 88.5 %reduce-scatter.4.cloned.1.call-done = f32[48,384]{1,0:T(8,128)} async-done(((f32[1536,384]{1,0:T(8,128)}), f32[48,384]{1,0:T(8,128)}) %reduce-scatter.4.cloned.1.call-update) | async-done | bytes 73744 | tf_op jit(solution)/shard_map/reduce_scatter | solution.py:98
  (74 shorter events, 15.7 us)
Async XLA Ops:
  7.2 200.7 %copy-start = (bf16[1536,384]{1,0:T(8,128)(2,1)S(1)}, bf16[1536,384]{1,0:T(8,128)(2,1)}, u32[]{:S(2)}) copy-start(bf16[1536,384]{1,0:T(8,128)(2,1)} %param.9) | copy-start | bytes 3538948
  7.2 54.9 %copy-start.17 = (s32[2]{0:T(128)S(1)}, s32[2]{0:T(128)}, u32[]{:S(2)}) copy-start(s32[2]{0:T(128)} %param.11) | copy-start | bytes 28
  7.2 50.6 %all-gather.4.cloned.1.call-start = ((), (), s32[]{:S(2)}) async-start(), calls=%async_computation.3 | async-start | bytes 3538944 | tf_op jit(solution)/shard_map/all_gather | solution.py:27
  7.9 123.8 %all-gather.6.cloned.1.call-start = ((), (), s32[]{:S(2)}) async-start(), calls=%async_computation.4 | async-start | bytes 3538944 | tf_op jit(solution)/shard_map/all_gather | solution.py:33
  60.2 13.9 %collective-permute-start = (bf16[8,32,1536]{2,1,0:T(8,128)(2,1)}, bf16[8,32,1536]{2,1,0:T(8,128)(2,1)S(1)}, u32[]{:S(2)}, u32[]{:S(2)}) collective-permute-start(bf16[8,32,1536]{2,1,0:T(8,128)(2,1)} %get-tuple-element.25), channel_id=1, source_target_pairs={{0,1},{1,2},{2,3},{3,4},{4,5},{5,6},{6,7},{7,8},{8,9},{9,10},{10,1... | collective-permute-start | bytes 2359304 | tf_op jit(solution)/shard_map/ppermute | solution.py:16
  67.0 7.2 copy-start.5
  67.0 13.4 %collective-permute-start.1 = (bf16[8,32,1536]{2,1,0:T(8,128)(2,1)S(1)}, bf16[8,32,1536]{2,1,0:T(8,128)(2,1)S(1)}, u32[]{:S(2)}, u32[]{:S(2)}) collective-permute-start(bf16[8,32,1536]{2,1,0:T(8,128)(2,1)S(1)} %get-tuple-element.24), channel_id=1, source_target_pairs={{1,0},{2,1},{3,2},{4,3},{5,4},{6,5},{7,6},{8,7},{9,8},{10,9},{11,1... | collective-permute-start | bytes 2359304 | tf_op jit(solution)/shard_map/ppermute | solution.py:17
  74.2 6.3 copy-start.18
  74.4 7.3 copy-start.16
  80.4 3.6 copy-start.7
  85.1 122.8 %all-gather.8.cloned.1.call-start = ((), (), s32[]{:S(2)}) async-start(), calls=%async_computation.5 | async-start | bytes 3538944 | tf_op jit(solution)/shard_map/all_gather | solution.py:83
  136.8 10.3 %copy-start.9 = (bf16[3,192,1536]{2,1,0:T(8,128)(2,1)S(1)}, bf16[3,192,1536]{2,1,0:T(8,128)(2,1)}, u32[]{:S(2)}) copy-start(bf16[3,192,1536]{2,1,0:T(8,128)(2,1)} %param.8) | copy-start | bytes 5308420
  139.5 13.6 %collective-permute-start.2 = (bf16[8,32,1536]{2,1,0:T(8,128)(2,1)}, bf16[8,32,1536]{2,1,0:T(8,128)(2,1)}, u32[]{:S(2)}, u32[]{:S(2)}) collective-permute-start(bf16[8,32,1536]{2,1,0:T(8,128)(2,1)} %get-tuple-element.22), channel_id=1, source_target_pairs={{0,1},{1,2},{2,3},{3,4},{4,5},{5,6},{6,7},{7,8},{8,9},{9,10},{10,1... | collective-permute-start | bytes 2359304 | tf_op jit(solution)/shard_map/ppermute | solution.py:16
  141.5 13.5 %collective-permute-start.3 = (bf16[8,32,1536]{2,1,0:T(8,128)(2,1)}, bf16[8,32,1536]{2,1,0:T(8,128)(2,1)}, u32[]{:S(2)}, u32[]{:S(2)}) collective-permute-start(bf16[8,32,1536]{2,1,0:T(8,128)(2,1)} %get-tuple-element.23), channel_id=1, source_target_pairs={{1,0},{2,1},{3,2},{4,3},{5,4},{6,5},{7,6},{8,7},{9,8},{10,9},{11,1... | collective-permute-start | bytes 2359304 | tf_op jit(solution)/shard_map/ppermute | solution.py:17
  147.1 7.8 copy-start.2
  156.5 3.6 copy-start.4
  161.2 174.1 %copy-start.8 = (s32[8,128,384]{2,1,0:T(8,128)S(1)}, s32[8,128,384]{2,1,0:T(8,128)}, u32[]{:S(2)}) copy-start(s32[8,128,384]{2,1,0:T(8,128)} %param.10) | copy-start | bytes 4718596
  161.2 360.9 %reduce-scatter.6.cloned.1.call-start = ((), (), s32[]{:S(2)}) async-start(), calls=%async_computation.7 | async-start | bytes 3538944 | tf_op jit(solution)/shard_map/reduce_scatter | solution.py:107
  463.6 2.1 copy-start.14
  475.7 46.4 %copy-start.12 = (f32[8,128,192]{1,2,0:T(8,128)S(1)}, f32[8,128,192]{1,2,0:T(8,128)}, u32[]{:S(2)}) copy-start(f32[8,128,192]{1,2,0:T(8,128)} %get-tuple-element.33) | copy-start | bytes 2359300
  475.7 53.9 %copy-start.10 = (bf16[3,192,1536]{2,1,0:T(8,128)(2,1)S(1)}, bf16[3,192,1536]{2,1,0:T(8,128)(2,1)}, u32[]{:S(2)}) copy-start(bf16[3,192,1536]{2,1,0:T(8,128)(2,1)} %param.8) | copy-start | bytes 5308420
  475.8 121.5 %reduce-scatter.8.cloned.1.call-start = ((), (), s32[]{:S(2)}) async-start(), calls=%async_computation.8 | async-start | bytes 3538944 | tf_op jit(solution)/shard_map/reduce_scatter | solution.py:124
  523.8 9.1 %collective-permute-start.4 = (bf16[8,32,192]{1,2,0:T(8,128)(2,1)S(1)}, bf16[8,32,192]{1,2,0:T(8,128)(2,1)S(1)}, u32[]{:S(2)}, u32[]{:S(2)}) collective-permute-start(bf16[8,32,192]{1,2,0:T(8,128)(2,1)S(1)} %get-tuple-element.26), channel_id=1, source_target_pairs={{0,1},{1,2},{2,3},{3,4},{4,5},{5,6},{6,7},{7,8},{8,9},{9,10},{10,1... | collective-permute-start | bytes 294920 | tf_op jit(solution)/shard_map/ppermute | solution.py:16
  525.8 8.9 %collective-permute-start.5 = (bf16[8,32,192]{1,2,0:T(8,128)(2,1)S(1)}, bf16[8,32,192]{1,2,0:T(8,128)(2,1)S(1)}, u32[]{:S(2)}, u32[]{:S(2)}) collective-permute-start(bf16[8,32,192]{1,2,0:T(8,128)(2,1)S(1)} %get-tuple-element.27), channel_id=1, source_target_pairs={{1,0},{2,1},{3,2},{4,3},{5,4},{6,5},{7,6},{8,7},{9,8},{10,9},{11,1... | collective-permute-start | bytes 294920 | tf_op jit(solution)/shard_map/ppermute | solution.py:17
  547.9 209.4 %all-reduce.6.cloned.1.call-start = ((), (), s32[]{:S(2)}) async-start(), calls=%async_computation.9 | async-start | bytes 25165824
  551.1 3.2 copy-start.3
  557.2 40.1 %copy-start.11 = (bf16[8,128,192]{1,0,2:T(8,128)(2,1)S(1)}, bf16[8,128,192]{1,0,2:T(8,128)(2,1)}, u32[]{:S(2)}) copy-start(bf16[8,128,192]{1,0,2:T(8,128)(2,1)} %reduce-scatter.6.cloned.1.call-done) | copy-start | bytes 1179652
  557.2 40.1 %copy-start.13 = (f32[8,128,192]{1,2,0:T(8,128)S(1)}, f32[8,128,192]{1,2,0:T(8,128)}, u32[]{:S(2)}) copy-start(f32[8,128,192]{1,2,0:T(8,128)} %get-tuple-element.31) | copy-start | bytes 2359300
  601.9 3.2 copy-start.6
  614.6 1.1 copy-start.15
  614.6 6.4 copy-start.19
  614.6 233.7 %reduce-scatter.4.cloned.1.call-start = ((), (), s32[]{:S(2)}) async-start(), calls=%async_computation.6 | async-start | bytes 2433024 | tf_op jit(solution)/shard_map/reduce_scatter | solution.py:98
  615.7 232.6 %copy-start.1 = (bf16[1536,384]{1,0:T(8,128)(2,1)S(1)}, bf16[1536,384]{1,0:T(8,128)(2,1)}, u32[]{:S(2)}) copy-start(bf16[1536,384]{1,0:T(8,128)(2,1)} %param.9) | copy-start | bytes 3538948
Sparse Core Ops, SparseCore 0:
  9.8 47.9 all-gather.3
  85.2 46.5 all-gather.5
  161.3 46.5 all-gather.7
  475.9 46.1 reduce-scatter.5
  548.0 49.2 reduce-scatter.7
  614.7 142.5 all-reduce.5
  761.7 86.5 reduce-scatter.3
where the time goes:
time: 856 us; the launch traced here: 855 us
  waiting for transfers between devices  461 us (54%)
  blocking collectives  246 us (29%)
  local copies, waits for them, and re-layouts  53.6 us (6%)
  matrix products  43.2 us (5%)
  between operations  19.1 us (2%)
  starting transfers between devices  17.7 us (2%)
  other arithmetic  13.6 us (2%)
    unnamed x8, waiting for transfers between devices  136 us
    psum x1, blocking collectives, on_device(): lax.psum((exp_local, count_local, cross_local), 'seq')  124 us
    pmax x1, blocking collectives, on_device(): peak_all = lax.pmax(local_peak, 'seq')  122 us
    reduce_scatter x1, waiting for transfers between devices, on_device(): lax.psum_scatter(jnp.einsum('blc,blt->ct', head_rows, logit_grad, preferr...  88.5 us
    all_gather x1, waiting for transfers between devices, framed_input(): gathered = lax.all_gather(block, 'dp', axis=0, tiled=True)  49.8 us
    all_gather x1, waiting for transfers between devices, framed_hidden(): gathered = lax.all_gather(block, 'dp', axis=2, tiled=True)  46.6 us
    all_gather x1, waiting for transfers between devices, on_device(): head_rows = lax.all_gather(hidden_two, 'dp', axis=2, tiled=True)  46.6 us
    reduce_scatter x1, waiting for transfers between devices, on_device(): lax.psum_scatter(back_partial.astype(jnp.bfloat16), 'dp', scatter_dimensi...  46.3 us
  transfers between devices with their start and end apart: 13, of which 12 were waited for; matrix products, arithmetic and copies ran while one was open for 4% of the time, Pallas kernels for 0%

commit v1 on v0

v1 whole, which is shorter than its diff:
```python
import functools

import jax
import jax.numpy as jnp
from jax import lax
from jax.experimental import pallas as pl
from jax.experimental.pallas import tpu as pltpu
from jax.sharding import PartitionSpec as P

DMAX = 32
NZ = 8
MESH = pl.DeviceIdType.MESH
BF = jnp.bfloat16
F32 = jnp.float32


def remote(src, dst, send, recv, device):
    return pltpu.make_async_remote_copy(
        src_ref=src, dst_ref=dst, send_sem=send, recv_sem=recv, device_id=device, device_id_type=MESH
    )


def greet(devices):
    barrier = pltpu.get_barrier_semaphore()
    for device in devices:
        pl.semaphore_signal(barrier, inc=1, device_id=device, device_id_type=MESH)
    pl.semaphore_wait(barrier, len(devices))


def z_neighbours():
    z = lax.axis_index("dp")
    return z, lax.rem(z + 1, NZ), lax.rem(z + NZ - 1, NZ)


def seq_neighbours():
    s, n = lax.axis_index("seq"), lax.axis_size("seq")
    return s, lax.rem(s + 1, n), lax.rem(s + n - 1, n)


def ring_gather(own, slot, half_rows, send_sem, recv_sem, on_block):
    z, right, left = z_neighbours()
    copies = {}
    for way in (0, 1):
        sign = -1 if way == 0 else 1
        peer = {"dp": right if way == 0 else left}
        for step in range(4):
            block = lax.rem(z + sign * step + NZ, NZ)
            for half in (0, 1):
                if step == 3 and half != way:
                    continue
                source = own(half) if step == 0 else slot(block, half)
                copies[way, step, half] = remote(
                    source, slot(block, half), send_sem.at[way, step, half], recv_sem.at[way, step, half], peer
                )
    for half in (0, 1):
        for way in (0, 1):
            copies[way, 0, half].start()
    on_block(0, z)
    for step in (1, 2, 3):
        for half in (0, 1):
            for way in (0, 1):
                copies[way, step - 1, half].wait_recv()
                if (way, step, half) in copies:
                    copies[way, step, half].start()
        on_block(2 * step - 1, lax.rem(z - step + NZ, NZ))
        on_block(2 * step, lax.rem(z + step, NZ))
    copies[0, 3, 0].wait_recv()
    copies[1, 3, 1].wait_recv()
    on_block(7, lax.rem(z + 4, NZ))
    for copy in copies.values():
        copy.wait_send()


def rows_gather_kernel(x_ref, out_ref, send_sem, recv_sem, edge_send, edge_recv, own_sem):
    length = x_ref.shape[0]
    z, right, left = z_neighbours()
    s, after, before = seq_neighbours()
    greet([{"dp": right}, {"dp": left}, {"seq": after}, {"seq": before}])
    mine = pltpu.make_async_copy(x_ref, out_ref.at[z, pl.ds(DMAX, length)], own_sem)
    mine.start()
    half_rows = length // 2
    edges = []

    def on_block(order, block):
        if order == 0:
            first, last = x_ref.at[pl.ds(0, DMAX)], x_ref.at[pl.ds(length - DMAX, DMAX)]
        else:
            first, last = out_ref.at[block, pl.ds(DMAX, DMAX)], out_ref.at[block, pl.ds(length, DMAX)]
        for side, (src, dst, peer) in enumerate(
            (
                (last, out_ref.at[block, pl.ds(0, DMAX)], after),
                (first, out_ref.at[block, pl.ds(DMAX + length, DMAX)], before),
            )
        ):
            copy = remote(src, dst, edge_send.at[side, order], edge_recv.at[side, order], {"seq": peer})
            copy.start()
            edges.append(copy)

    ring_gather(
        lambda h: x_ref.at[pl.ds(h * half_rows, half_rows)],
        lambda k, h: out_ref.at[k, pl.ds(DMAX + h * half_rows, half_rows)],
        half_rows,
        send_sem,
        recv_sem,
        on_block,
    )
    for copy in edges:
        copy.wait_recv()
        copy.wait_send()
    mine.wait()

    @pl.when(s == 0)
    def _():
        out_ref[:, 0:DMAX, :] = jnp.zeros_like(out_ref[:, 0:DMAX, :])

    @pl.when(s == lax.axis_size("seq") - 1)
    def _():
        out_ref[:, length + DMAX :, :] = jnp.zeros_like(out_ref[:, length + DMAX :, :])


def whole(n):
    return [pl.BlockSpec(memory_space=pltpu.VMEM)] * n


def rows_gather(x, collective_id):
    length, width = x.shape
    return pl.pallas_call(
        rows_gather_kernel,
        out_shape=jax.ShapeDtypeStruct((NZ, length + 2 * DMAX, width), x.dtype),
        in_specs=whole(1),
        out_specs=whole(1)[0],
        scratch_shapes=[
            pltpu.SemaphoreType.DMA((2, 4, 2)),
            pltpu.SemaphoreType.DMA((2, 4, 2)),
            pltpu.SemaphoreType.DMA((2, 8)),
            pltpu.SemaphoreType.DMA((2, 8)),
            pltpu.SemaphoreType.DMA,
        ],
        compiler_params=pltpu.CompilerParams(collective_id=collective_id, has_side_effects=True),
        name="rows_gather",
    )(x)


LO, HI = slice(0, 64), slice(64, 128)


def chan_gather_kernel(framed, x_ref, out_ref, held, edge, send_sem, recv_sem, edge_send, edge_recv):
    rows = x_ref.shape[0]
    part = rows // 2
    rim = 8 * DMAX
    base = rim if framed else 0
    z, right, left = z_neighbours()
    s, after, before = seq_neighbours()
    held[z, 0:rows, :] = x_ref[:, 0:128]
    held[z, rows : rows + part, :] = jnp.concatenate([x_ref[0:part, 128:192], x_ref[part:rows, 128:192]], axis=1)
    peers = [{"dp": right}, {"dp": left}]
    if framed:
        peers += [{"seq": after}, {"seq": before}]
    greet(peers)
    half_rows = (rows + part) // 2
    edges = []

    def on_block(order, block):
        if not framed:
            return
        for side, piece, start, peer in (
            (0, 0, rows - rim, after),
            (0, 1, rows + part - rim, after),
            (1, 0, 0, before),
            (1, 1, rows, before),
        ):
            copy = remote(
                held.at[block, pl.ds(start, rim)],
                edge.at[side, block, pl.ds(piece * rim, rim)],
                edge_send.at[side, piece, order],
                edge_recv.at[side, piece, order],
                {"seq": peer},
            )
            copy.start()
            edges.append(copy)

    ring_gather(
        lambda h: held.at[z, pl.ds(h * half_rows, half_rows)],
        lambda k, h: held.at[k, pl.ds(h * half_rows, half_rows)],
        half_rows,
        send_sem,
        recv_sem,
        on_block,
    )
    for j in range(NZ // 2):
        one, two, lane = 2 * j, 2 * j + 1, 384 * j
        out_ref[base : base + rows, lane : lane + 128] = held[one, 0:rows, :]
        out_ref[base : base + rows, lane + 256 : lane + 384] = held[two, 0:rows, :]
        for h, lanes in ((0, LO), (1, HI)):
            out_ref[base + h * part : base + (h + 1) * part, lane + 128 : lane + 256] = jnp.concatenate(
                [held[one, rows : rows + part, lanes], held[two, rows : rows + part, lanes]], axis=1
            )
    if framed:
        for copy in edges:
            copy.wait_recv()
            copy.wait_send()
        n = lax.axis_size("seq")
        for side, at, lanes, keep in ((0, 0, HI, s > 0), (1, base + rows, LO, s < n - 1)):
            for j in range(NZ // 2):
                one, two, lane = 2 * j, 2 * j + 1, 384 * j
                pieces = (
                    edge[side, one, 0:rim, :],
                    jnp.concatenate([edge[side, one, rim : 2 * rim, lanes], edge[side, two, rim : 2 * rim, lanes]], axis=1),
                    edge[side, two, 0:rim, :],
                )
                for i, piece in enumerate(pieces):
                    out_ref[at : at + rim, lane + 128 * i : lane + 128 * (i + 1)] = jnp.where(
                        keep, piece, jnp.zeros_like(piece)
                    )


def chan_gather(x, framed, collective_id):
    rows = x.shape[0]
    rim = 8 * DMAX
    return pl.pallas_call(
        functools.partial(chan_gather_kernel, framed),
        out_shape=jax.ShapeDtypeStruct((rows + (2 * rim if framed else 0), 192 * NZ), x.dtype),
        in_specs=whole(1),
        out_specs=whole(1)[0],
        scratch_shapes=[
            pltpu.VMEM((NZ, rows + rows // 2, 128), x.dtype),
            pltpu.VMEM((2, NZ, 2 * rim, 128) if framed else (1, 1, 16, 128), x.dtype),
            pltpu.SemaphoreType.DMA((2, 4, 2)),
            pltpu.SemaphoreType.DMA((2, 4, 2)),
            pltpu.SemaphoreType.DMA((2, 2, 8)),
            pltpu.SemaphoreType.DMA((2, 2, 8)),
        ],
        compiler_params=pltpu.CompilerParams(collective_id=collective_id, has_side_effects=True),
        name="chan_gather",
    )(x)


def chan_scatter_kernel(p_ref, out_ref, own, got, sent, send_sem, recv_sem):
    rows = p_ref.shape[0]
    part = rows // 2
    half_rows = (rows + part) // 2
    z, right, left = z_neighbours()
    for j in range(NZ // 2):
        one, two, lane = 2 * j, 2 * j + 1, 384 * j
        own[one, 0:rows, :] = p_ref[:, lane : lane + 128]
        own[two, 0:rows, :] = p_ref[:, lane + 256 : lane + 384]
        for block, lanes in ((one, slice(lane + 128, lane + 192)), (two, slice(lane + 192, lane + 256))):
            own[block, rows : rows + part, :] = jnp.concatenate([p_ref[0:part, lanes], p_ref[part:rows, lanes]], axis=1)
    greet([{"dp": right}, {"dp": left}])
    piece = lambda h: pl.ds(h * half_rows, half_rows)
    copies = {}
    for step in range(4):
        for half in (0, 1):
            for way in (0, 1):
                if step == 0 and half != way:
                    continue
                sign = 1 if way == 0 else -1
                block = lax.rem(z + sign * (4 - step) + NZ, NZ)
                before = copies.get((way, step - 1, half))
                if before is None:
                    source = own.at[block, piece(half)]
                else:
                    before.wait_recv()
                    sent[way, step - 1, piece(half), :] = (
                        got[way, step - 1, piece(half), :].astype(F32) + own[block, piece(half), :].astype(F32)
                    ).astype(BF)
                    source = sent.at[way, step - 1, piece(half)]
                copy = remote(
                    source,
                    got.at[way, step, piece(half)],
                    send_sem.at[way, step, half],
                    recv_sem.at[way, step, half],
                    {"dp": right if way == 0 else left},
                )
                copy.start()
                copies[way, step, half] = copy
    for half in (0, 1):
        copies[0, 3, half].wait_recv()
        copies[1, 3, half].wait_recv()

    def total(at, size):
        return (
            own[z, at : at + size, :].astype(F32)
            + got[0, 3, at : at + size, :].astype(F32)
            + got[1, 3, at : at + size, :].astype(F32)
        )

    out_ref[:, 0:128] = total(0, rows)
    rest = total(rows, part)
    out_ref[0:part, 128:192] = rest[:, LO]
    out_ref[part:rows, 128:192] = rest[:, HI]
    for copy in copies.values():
        copy.wait_send()


def chan_scatter(partial, collective_id):
    rows = partial.shape[0]
    block = (rows + rows // 2, 128)
    return pl.pallas_call(
        chan_scatter_kernel,
        out_shape=jax.ShapeDtypeStruct((rows, 192), F32),
        in_specs=whole(1),
        out_specs=whole(1)[0],
        scratch_shapes=[
            pltpu.VMEM((NZ, *block), BF),
            pltpu.VMEM((2, 4, *block), BF),
            pltpu.VMEM((2, 3, *block), BF),
            pltpu.SemaphoreType.DMA((2, 4, 2)),
            pltpu.SemaphoreType.DMA((2, 4, 2)),
        ],
        compiler_params=pltpu.CompilerParams(collective_id=collective_id, has_side_effects=True),
        name="chan_scatter",
    )(partial)


def seq_place():
    s = lax.axis_index("seq")
    return s // 8, lax.rem(s // 2, 4), lax.rem(s, 2)


def seq_peers():
    y, x, core = seq_place()
    at = lambda y, x, core: (y * 4 + x) * 2 + core
    other = at(y, x, 1 - core)
    along_x = [at(y, lax.rem(x + d, 4), core) for d in (1, 2, 3)]
    along_y = [at(lax.rem(y + d, 4), x, core) for d in (1, 2, 3)]
    return other, along_x, along_y


def stats_kernel(x_ref, out_ref, merged, got, send_sem, recv_sem, own_sem):
    y, x, core = seq_place()
    other, along_x, along_y = seq_peers()
    greet([{"seq": p} for p in [other, *along_x, *along_y]])
    stages = ((2, core, [other]), (4, x, along_x), (4, y, along_y))
    base = 0
    for number, (count, place, peers) in enumerate(stages):
        source = x_ref if number == 0 else merged.at[number - 1]
        copies = []
        for d, peer in enumerate(peers):
            copy = remote(
                source,
                got.at[number, place],
                send_sem.at[number, d],
                recv_sem.at[number, d],
                {"seq": peer},
            )
            copy.start()
            copies.append(copy)
        mine = pltpu.make_async_copy(source, got.at[number, place], own_sem.at[number])
        mine.start()
        mine.wait()
        for copy in copies:
            copy.wait_recv()
        peak = got[number, 0, 0]
        for i in range(1, count):
            peak = jnp.maximum(peak, got[number, i, 0])
        sums = [jnp.zeros_like(peak) for _ in range(3)]
        for i in range(count):
            sums[0] = sums[0] + got[number, i, 1] * jnp.exp(got[number, i, 0] - peak)
            sums[1] = sums[1] + got[number, i, 2]
            sums[2] = sums[2] + got[number, i, 3]
        for copy in copies:
            copy.wait_send()
        target = out_ref if number == 2 else merged.at[number]
        target[0] = peak
        for i in range(3):
            target[i + 1] = sums[i]


def merge_stats(stats, collective_id):
    shape = stats.shape
    return pl.pallas_call(
        stats_kernel,
        out_shape=jax.ShapeDtypeStruct(shape, F32),
        in_specs=whole(1),
        out_specs=whole(1)[0],
        scratch_shapes=[
            pltpu.VMEM((2, *shape), F32),
            pltpu.VMEM((3, 4, *shape), F32),
            pltpu.SemaphoreType.DMA((3, 3)),
            pltpu.SemaphoreType.DMA((3, 3)),
            pltpu.SemaphoreType.DMA((3,)),
        ],
        compiler_params=pltpu.CompilerParams(collective_id=collective_id, has_side_effects=True),
        name="merge_stats",
    )(stats)


def seq_scatter_kernel(
    x_ref, out_ref, pair, both, got_one, mid_one, got_two, sems_send, sems_recv, pair_send, pair_recv
):
    y, x, core = seq_place()
    other, along_x, along_y = seq_peers()
    rows = x_ref.shape[2]
    half = rows // 2
    greet([{"seq": p} for p in [other, *along_x, *along_y]])
    pairs = []
    for h in (0, 1):
        for q in range(4):
            copy = remote(
                x_ref.at[1 - core, pl.ds(4 * q, 4), pl.ds(h * half, half)],
                pair.at[h, pl.ds(4 * q, 4)],
                pair_send.at[h, q],
                pair_recv.at[h, q],
                {"seq": other},
            )
            copy.start()
            pairs.append(copy)
    copies = {}
    for h in (0, 1):
        for q in range(4):
            pairs[4 * h + q].wait_recv()

            @pl.loop(4 * q, 4 * q + 4)
            def _(i):
                total = pair[h, i].astype(F32) + x_ref[core, i, pl.ds(h * half, half), :].astype(F32)
                spot = lax.rem(i, 4) * 4 + i // 4 if h == 0 else i
                both[h, spot] = total.astype(BF)

        place, peers = (x, along_x) if h == 0 else (y, along_y)
        for d, peer in enumerate(peers):
            target = lax.rem(place + d + 1, 4)
            copy = remote(
                both.at[h, pl.ds(4 * target, 4)],
                got_one.at[h, 2 - d],
                sems_send.at[h, 0, d],
                sems_recv.at[h, 0, d],
                {"seq": peer},
            )
            copy.start()
            copies[h, 0, d] = copy
    for h in (0, 1):
        place = x if h == 0 else y
        for d in range(3):
            copies[h, 0, d].wait_recv()

        @pl.loop(0, 4)
        def _(i):
            total = both[h, 4 * place + i].astype(F32)
            for d in range(3):
                total = total + got_one[h, d, i].astype(F32)
            mid_one[h, i] = total.astype(BF)

        place, peers = (y, along_y) if h == 0 else (x, along_x)
        for d, peer in enumerate(peers):
            target = lax.rem(place + d + 1, 4)
            copy = remote(
                mid_one.at[h, target],
                got_two.at[h, 2 - d],
                sems_send.at[h, 1, d],
                sems_recv.at[h, 1, d],
                {"seq": peer},
            )
            copy.start()
            copies[h, 1, d] = copy
    for h in (0, 1):
        place = y if h == 0 else x
        for d in range(3):
            copies[h, 1, d].wait_recv()
        total = mid_one[h, place].astype(F32)
        for d in range(3):
            total = total + got_two[h, d].astype(F32)
        out_ref[h * half : (h + 1) * half, :] = total
    for copy in pairs:
        copy.wait_send()
    for copy in copies.values():
        copy.wait_send()


def seq_scatter(packed, collective_id):
    rows = packed.shape[2]
    half = rows // 2
    return pl.pallas_call(
        seq_scatter_kernel,
        out_shape=jax.ShapeDtypeStruct((rows, 128), F32),
        in_specs=whole(1),
        out_specs=whole(1)[0],
        scratch_shapes=[
            pltpu.VMEM((2, 16, half, 128), BF),
            pltpu.VMEM((2, 16, half, 128), BF),
            pltpu.VMEM((2, 3, 4, half, 128), BF),
            pltpu.VMEM((2, 4, half, 128), BF),
            pltpu.VMEM((2, 3, half, 128), BF),
            pltpu.SemaphoreType.DMA((2, 2, 3)),
            pltpu.SemaphoreType.DMA((2, 2, 3)),
            pltpu.SemaphoreType.DMA((2, 4)),
            pltpu.SemaphoreType.DMA((2, 4)),
        ],
        compiler_params=pltpu.CompilerParams(collective_id=collective_id, has_side_effects=True),
        name="seq_scatter",
    )(packed)


def activate(value):
    return jax.nn.gelu(value)


def shifted_taps(padded, spacing, length, sign):
    return [
        lax.dynamic_slice_in_dim(padded, DMAX + sign * (tap_index - 1) * spacing, length, 0) for tap_index in range(3)
    ]


def conv_apply(padded, weight, spacing, length):
    running = None
    for tap_index, rows in enumerate(shifted_taps(padded, spacing, length, 1)):
        term = jnp.einsum(
            "lc,dc->ld", rows.reshape(-1, rows.shape[2]), weight[tap_index], preferred_element_type=F32
        )
        running = term if running is None else running + term
    return running


def weight_grad(padded, upstream, spacing, length):
    return jnp.stack(
        [
            jnp.einsum("lc,ld->cd", rows.reshape(-1, rows.shape[2]), upstream, preferred_element_type=F32)
            for rows in shifted_taps(padded, spacing, length, 1)
        ]
    )


def seq_halo(value, width):
    size, length = lax.axis_size("seq"), value.shape[0]
    up = [(i, i + 1) for i in range(size - 1)]
    down = [(j, i) for i, j in up]
    before = lax.ppermute(value[length - width :], "seq", up)
    after = lax.ppermute(value[:width], "seq", down)
    return jnp.concatenate([before, value, after], axis=0)


def pack_head(grad):
    return grad.reshape(32, 48, 3, 128).transpose(0, 2, 1, 3).reshape(32, 144, 128).astype(BF)


def pack_conv(grad):
    blocks = grad.astype(BF).reshape(3, 32, 48, 192).transpose(1, 0, 2, 3).reshape(32, 144, 192)
    rest = jnp.concatenate([blocks[:, 0:72, 128:], blocks[:, 72:, 128:]], axis=2)
    return jnp.concatenate([blocks[:, :, :128], rest], axis=1)


def unpack_conv(block, odd):
    rest = jnp.concatenate([block[144:, 0:64], block[144:, 64:]], axis=0)
    main = block[:144]
    even_form = jnp.concatenate([main, rest], axis=1)
    odd_form = jnp.concatenate([rest, main], axis=1)
    return jnp.where(odd, odd_form, even_form).reshape(3, 48, 192)


def on_device(embeddings, conv_one, conv_two, head_weight, counts, dilation):
    length = embeddings.shape[1]
    chan_dev = conv_one.shape[1]
    own_index = lax.axis_index("dp")
    odd = lax.rem(own_index, 2) == 1
    turn = lambda w: jnp.where(odd, jnp.concatenate([w[:, 64:], w[:, :64]], axis=1), w)
    w_one, w_two = turn(conv_one), turn(conv_two)
    first_gap, second_gap = dilation[0], dilation[1]
    framed_in = jnp.transpose(rows_gather(embeddings[0], 0), (1, 0, 2))
    pre_one = conv_apply(framed_in, w_one, first_gap, length)
    centre_in = lax.slice_in_dim(framed_in, DMAX, DMAX + length, axis=0).reshape(-1, framed_in.shape[2])
    own_in = lax.dynamic_slice_in_dim(centre_in, own_index * chan_dev, chan_dev, 1)
    own_in = jnp.where(odd, jnp.concatenate([own_in[:, 64:], own_in[:, :64]], axis=1), own_in)
    hidden_one = (own_in.astype(F32) + activate(pre_one)).astype(BF)
    framed_one = chan_gather(hidden_one, True, 1).reshape(length + 2 * DMAX, NZ, -1)
    pre_two = conv_apply(framed_one, w_two, second_gap, length)
    hidden_two = (hidden_one.astype(F32) + activate(pre_two)).astype(BF)
    head_rows = chan_gather(hidden_two, False, 2)
    logits = jnp.einsum("lc,ct->lt", head_rows, head_weight, preferred_element_type=F32)
    logits = logits.reshape(length, NZ, -1)
    targets = jnp.transpose(counts, (1, 0, 2)).astype(F32)
    local_peak = jnp.max(logits, axis=0)
    stats = jnp.stack(
        [
            local_peak,
            jnp.sum(jnp.exp(logits - local_peak[None]), axis=0),
            jnp.sum(targets, axis=0),
            jnp.sum(targets * logits, axis=0),
        ]
    )
    peak_all, exp_total, count_total, cross_total = merge_stats(stats, 3)
    all_bins = length * lax.axis_size("seq")
    log_total = peak_all + jnp.log(exp_total)
    track_loss = (count_total * log_total - cross_total) / all_bins
    logit_grad = ((count_total[None] * jnp.exp(logits - log_total[None]) - targets) / all_bins).astype(BF)
    logit_grad = logit_grad.reshape(length * NZ, -1)
    grad_head = jnp.einsum("lc,lt->ct", head_rows, logit_grad, preferred_element_type=F32)
    back_partial = jnp.einsum("lt,ct->lc", logit_grad, head_weight, preferred_element_type=F32).astype(BF)
    grad_two_out = chan_scatter(back_partial, 4)
    upstream_two = jax.vjp(activate, pre_two)[1](grad_two_out)[0].astype(BF)
    grad_two = weight_grad(framed_one, upstream_two, second_gap, length)
    framed_back = seq_halo(upstream_two.reshape(length, NZ, -1), DMAX)
    conv_partial = None
    for tap_index, rows in enumerate(shifted_taps(framed_back, second_gap, length, -1)):
        term = jnp.einsum("ld,dc->lc", rows.reshape(length * NZ, -1), w_two[tap_index], preferred_element_type=F32)
        conv_partial = term if conv_partial is None else conv_partial + term
    grad_one_out = grad_two_out + chan_scatter(conv_partial.astype(BF), 5)
    upstream_one = jax.vjp(activate, pre_one)[1](grad_one_out)[0].astype(BF)
    grad_one = weight_grad(framed_in, upstream_one, first_gap, length)
    packed = jnp.concatenate([pack_head(grad_head), pack_conv(grad_two), pack_conv(grad_one)], axis=1)
    packed = packed.reshape(16, 2, 576, 128).transpose(1, 0, 2, 3)
    summed = seq_scatter(packed, 6)
    out_head = summed[:144].reshape(3, 48, 128).transpose(1, 0, 2).reshape(48, 384)
    return (
        track_loss,
        out_head,
        unpack_conv(summed[360:576], odd),
        unpack_conv(summed[144:360], odd),
    )


def solution(mesh):
    placed = (
        P("dp", "seq", None),
        P(None, "dp", None),
        P(None, "dp", None),
        P(None, "dp"),
        P(None, "seq", "dp"),
        P(),
    )
    return jax.shard_map(
        on_device,
        mesh=mesh,
        in_specs=placed,
        out_specs=(P(None, "dp"), P("seq", "dp"), P(None, "seq", "dp"), P(None, "seq", "dp")),
        check_vma=False,
    )
```

time: 856 us -> 418 us (0.49)
  waiting for transfers between devices: 461 us -> 0.01 us
  Pallas kernels: 0 us -> 253 us
  blocking collectives: 246 us -> 0 us
  local copies, waits for them, and re-layouts: 53.6 us -> 76.5 us
  between operations: 19.1 us -> 5.35 us
  starting transfers between devices: 17.7 us -> 4.78 us
    pallas_call x0 -> x7, Pallas kernels: none -> 253 us  [the longest x2 84 us: chan_gather(): pl.pallas_call(functools.partial(chan_gather_kernel, framed), out_shape=j...]
    reduce_scatter x3 -> x0, waiting for transfers between devices: 168 us -> none  [the longest x1 88.5 us: on_device(): lax.psum_scatter(jnp.einsum('blc,blt->ct', head_rows, logit_grad, preferr...]
    all_gather x3 -> x0, waiting for transfers between devices: 143 us -> none  [the longest x1 49.8 us: framed_input(): gathered = lax.all_gather(block, 'dp', axis=0, tiled=True)]
    unnamed x8 -> x0, waiting for transfers between devices: 136 us -> none
    psum x1 -> x0, blocking collectives: 124 us -> none  [on_device(): lax.psum((exp_local, count_local, cross_local), 'seq')]
    pmax x1 -> x0, blocking collectives: 122 us -> none  [on_device(): peak_all = lax.pmax(local_peak, 'seq')]
    dot_general x0 -> x9, local copies, waits for them, and re-layouts: none -> 38.3 us  [the longest x7 31.2 us: weight_grad(): jnp.einsum('lc,ld->cd', rows.reshape(-1, rows.shape[2]), upstream, prefer...]
    convert_element_type x4 -> x1, local copies, waits for them, and re-layouts: 22.2 us -> 2.47 us  [on_device(): hidden_one = (own_in.astype(F32) + activate(pre_one)).astype(BF)]
  transfers between devices with their start and end apart: 13 -> 2, of which waited for: 12 -> 0; matrix products, arithmetic and copies ran while one was open for 4% -> 15% of each run, Pallas kernels for 0% -> 0%
where the time goes in v1:
time: 418 us; the launch traced here: 411 us
  Pallas kernels  253 us (61%)
  local copies, waits for them, and re-layouts  76.5 us (18%)
  matrix products  50.4 us (12%)
  other arithmetic  21.4 us (5%)
  between operations  5.35 us (1%)
  starting transfers between devices  4.78 us (1%)
    pallas_call x2, Pallas kernels, chan_gather(): pl.pallas_call(functools.partial(chan_gather_kernel, framed), out_shape=j...  84 us
    pallas_call x2, Pallas kernels, chan_scatter(): pl.pallas_call(chan_scatter_kernel, out_shape=jax.ShapeDtypeStruct((rows,...  75.3 us
    pallas_call x1, Pallas kernels, rows_gather(): pl.pallas_call(rows_gather_kernel, out_shape=jax.ShapeDtypeStruct((NZ, le...  44.6 us
    pallas_call x1, Pallas kernels, seq_scatter(): pl.pallas_call(seq_scatter_kernel, out_shape=jax.ShapeDtypeStruct((rows,...  33.1 us
    dot_general x7, local copies, waits for them, and re-layouts, weight_grad(): jnp.einsum('lc,ld->cd', rows.reshape(-1, rows.shape[2]), upstream, prefer...  31.2 us
    dot_general x6, matrix products, conv_apply(): jnp.einsum('lc,dc->ld', rows.reshape(-1, rows.shape[2]), weight[tap_index...  16.4 us
    pallas_call x1, Pallas kernels, merge_stats(): pl.pallas_call(stats_kernel, out_shape=jax.ShapeDtypeStruct(shape, F32),...  15.6 us
    dot_general x6, matrix products, weight_grad(): jnp.einsum('lc,ld->cd', rows.reshape(-1, rows.shape[2]), upstream, prefer...  13.7 us
  transfers between devices with their start and end apart: 2, of which 0 were waited for; matrix products, arithmetic and copies ran while one was open for 15% of the time, Pallas kernels for 0%

profile of v1, /device:TPU:2, one launch (start us, length us, event | category | flops | bytes accessed | tf_op | source)
XLA Modules:
  0.0 411.0 jit_solution(14864236636595935672)
XLA Ops:
  0.7 44.6 %rows_gather.1 = bf16[8,192,1536]{2,1,0:T(8,128)(2,1)} custom-call(bf16[128,1536]{1,0:T(8,128)(2,1)} %bitcast.248), custom_call_target="tpu_custom_call" | custom-call | tf_op jit(solution)/shard_map/rows_gather/pallas_call | solution.py:127
  45.2 2.1 slice.140
  47.3 1.7 copy-done.6
  49.1 3.4 copy.184
  52.5 1.4 constant_dynamic-slice_fusion
  55.5 1.5 copy-done.14
  62.6 2.2 fusion.68
  64.7 2.5 copy.112
  67.2 4.1 maximum_select_fusion
  71.3 1.9 convolution_bitcast_fusion
  73.2 5.7 %dynamic-slice_bitcast_fusion = (bf16[128,8,1536]{2,0,1:T(8,128)(2,1)S(1)}, bf16[128,8,1536]{2,0,1:T(8,128)(2,1)S(1)}) fusion(bf16[8,192,1536]{2,1,0:T(8,128)(2,1)} %rows_gather.1, s32[]{:T(128)S(6)} %select_n.61, s32[]{:T(128)S(6)} %select_n.58), kind=kLoop, calls=%fused_computation.12 | loop fusion | bytes 12582920 | tf_op jit(solution)/shard_map/dynamic_slice | solution.py:500
  78.9 1.9 fusion.30
  81.6 3.2 add_convert_fusion.2
  84.8 44.0 %chan_gather.2 = bf16[1536,1536]{1,0:T(8,128)(2,1)} custom-call(bf16[1024,192]{1,0:T(8,128)(2,1)} %get-tuple-element.28.x_ref), custom_call_target="tpu_custom_call" | custom-call | tf_op jit(solution)/shard_map/chan_gather/pallas_call | solution.py:220
  128.8 3.0 fusion.2
  132.1 2.0 fusion.27
  134.0 4.5 %add_convert_fusion.1 = (bf16[1024,192]{1,0:T(8,128)(2,1)}, f32[1024,192]{1,0:T(8,128)}) fusion(bf16[1024,192]{1,0:T(8,128)(2,1)S(1)} %copy-done.25, f32[1024,192]{1,0:T(8,128)} %fusion.27, bf16[3,192,1536]{2,1,0:T(8,128)(2,1)S(1)} %copy-done.15, bf16[192,8,1536]{2,1,0:T(8,128)(2,1)} %bitcast.224, s32[]{:T(128)S(6)} %select_n.64), kind=kOutput, calls=%fused_computation.81 | convolution fusion | flops 606339072 | bytes 6488068 | tf_op jit(solution)/shard_map/lc,dc->ld/dot_general | solution.py:507
  138.6 40.0 %chan_gather.3 = bf16[1024,1536]{1,0:T(8,128)(2,1)} custom-call(bf16[1024,192]{1,0:T(8,128)(2,1)} %get-tuple-element.30.x_ref), custom_call_target="tpu_custom_call" | custom-call | tf_op jit(solution)/shard_map/chan_gather/pallas_call | solution.py:220
  178.6 3.8 bitcast_reduce_fusion.1
  185.3 15.6 %merge_stats.1 = f32[4,8,384]{2,1,0:T(8,128)} custom-call(f32[4,8,384]{2,1,0:T(8,128)} %pad_maximum_fusion.3.x_ref), custom_call_target="tpu_custom_call" | custom-call | tf_op jit(solution)/shard_map/merge_stats/pallas_call | solution.py:372
  201.0 1.4 fusion.69
  203.1 5.4 %convolution_convert_fusion.p_ref = bf16[1024,1536]{1,0:T(8,128)(2,1)} fusion(bf16[1536,384]{1,0:T(8,128)(2,1)S(1)} %copy-done, f32[1024,384]{1,0:T(8,128)} %copy-done.4, s32[8,128,384]{2,1,0:T(8,128)S(1)} %copy-done.3, f32[8,384]{1,0:T(8,128)S(1)} %get-tuple-element.8, f32[8,384]{1,0:T(8,128)S(1)} %slice_bitcast_fusion.17), kind=kOutput, calls=%fused_computation.2 | convolution fusion | flops 1211891712 | bytes 7495680 | tf_op jit(solution)/shard_map/lt,ct->lc/dot_general | solution.py:587
  208.5 36.4 %chan_scatter.2 = f32[1024,192]{1,0:T(8,128)} custom-call(bf16[1024,1536]{1,0:T(8,128)(2,1)} %convolution_convert_fusion.p_ref), custom_call_target="tpu_custom_call" | custom-call | tf_op jit(solution)/shard_map/chan_scatter/pallas_call | solution.py:299
  244.9 2.4 fusion.56
  248.0 1.9 collective-permute-start.1
  249.9 2.9 collective-permute-start
  252.8 2.0 fusion.91
  254.8 6.0 %dynamic-slice_bitcast_fusion.3 = (bf16[1536,1024]{0,1:T(8,128)(2,1)}, bf16[1536,1024]{0,1:T(8,128)(2,1)}) fusion(bf16[192,8,1536]{2,1,0:T(8,128)(2,1)} %bitcast.225, s32[]{:T(128)S(6)} %select_n.62, s32[]{:T(128)S(6)} %select_n.64), kind=kLoop, calls=%fused_computation.24 | loop fusion | bytes 12582920 | tf_op jit(solution)/shard_map/lc,ld->cd/dot_general | solution.py:517
  263.7 6.1 %copy_bitcast_fusion.2 = (bf16[1536,1024]{0,1:T(8,128)(2,1)}, bf16[1536,1024]{0,1:T(8,128)(2,1)}) fusion(bf16[128,8,1536]{2,0,1:T(8,128)(2,1)S(1)} %copy-done.10, bf16[128,8,1536]{2,0,1:T(8,128)(2,1)S(1)} %copy-done.12), kind=kLoop, calls=%fused_computation.14 | loop fusion | bytes 12582912 | tf_op jit(solution)/shard_map/lc,ld->cd/dot_general | solution.py:517
  269.7 3.7 fusion.67
  273.4 4.8 %copy.117 = bf16[1536,1024]{1,0:T(8,128)(2,1)} copy(bf16[1536,1024]{0,1:T(8,128)(2,1)} %bitcast.229) | data formatting | bytes 6291456 | tf_op jit(solution)/shard_map/lc,lt->ct/dot_general | solution.py:586
  278.2 2.3 copy.118
  280.5 3.9 convolution_convert_fusion.2
  285.7 4.7 %copy.122 = bf16[1536,1024]{1,0:T(8,128)(2,1)} copy(bf16[1536,1024]{0,1:T(8,128)(2,1)} %get-tuple-element.10) | data formatting | bytes 6291456 | tf_op jit(solution)/shard_map/lc,ld->cd/dot_general | solution.py:517
  290.3 3.8 fusion.40
  295.2 4.7 %copy.119 = bf16[1536,1024]{1,0:T(8,128)(2,1)} copy(bf16[1536,1024]{0,1:T(8,128)(2,1)} %get-tuple-element.9) | data formatting | bytes 6291456 | tf_op jit(solution)/shard_map/lc,ld->cd/dot_general | solution.py:517
  299.9 3.0 fusion.39
  303.8 1.3 slice_dynamic-update-slice_fusion.1
  305.1 4.7 %copy.128 = bf16[1536,1024]{1,0:T(8,128)(2,1)} copy(bf16[1536,1024]{0,1:T(8,128)(2,1)} %get-tuple-element.36) | data formatting | bytes 6291456 | tf_op jit(solution)/shard_map/lc,ld->cd/dot_general | solution.py:517
  309.8 4.9 %copy.125 = bf16[1536,1024]{1,0:T(8,128)(2,1)} copy(bf16[1536,1024]{0,1:T(8,128)(2,1)} %get-tuple-element.37) | data formatting | bytes 6291456 | tf_op jit(solution)/shard_map/lc,ld->cd/dot_general | solution.py:517
  315.8 1.3 pad_maximum_fusion
  319.0 2.6 add_convert_fusion.p_ref
  321.7 38.9 %chan_scatter.3 = f32[1024,192]{1,0:T(8,128)} custom-call(bf16[1024,1536]{1,0:T(8,128)(2,1)} %add_convert_fusion.p_ref), custom_call_target="tpu_custom_call" | custom-call | tf_op jit(solution)/shard_map/chan_scatter/pallas_call | solution.py:299
  360.6 2.1 fusion.49
  362.8 2.1 fusion.19
  366.2 3.0 fusion.41
  371.0 2.5 copy.183
  373.5 33.1 %seq_scatter.1 = f32[576,128]{1,0:T(8,128)} custom-call(bf16[2,16,576,128]{3,2,1,0:T(8,128)(2,1)} %bitcast.228), custom_call_target="tpu_custom_call" | custom-call | tf_op jit(solution)/shard_map/seq_scatter/pallas_call | solution.py:473
  (107 shorter events, 25.3 us)
Async XLA Ops:
  0.6 178.0 %copy-start = (bf16[1536,384]{1,0:T(8,128)(2,1)S(1)}, bf16[1536,384]{1,0:T(8,128)(2,1)}, u32[]{:S(2)}) copy-start(bf16[1536,384]{1,0:T(8,128)(2,1)} %param.9) | copy-start | bytes 3538948
  47.3 1.7 copy-start.6
  54.0 1.5 copy-start.17
  55.5 1.5 copy-start.14
  55.5 2.6 copy-start.26
  57.0 10.3 %slice-start.6 = ((bf16[3,192,1536]{2,1,0:T(8,128)(2,1)}), bf16[3,64,1536]{2,1,0:T(8,128)(2,1)S(1)}, s32[]{:S(2)}) async-start(bf16[3,192,1536]{2,1,0:T(8,128)(2,1)} %param.7), calls=%async_computation.6 | async-start | bytes 1179648 | tf_op jit(solution)/shard_map/slice | solution.py:555
  57.0 10.3 %slice-start.7 = ((bf16[3,192,1536]{2,1,0:T(8,128)(2,1)}), bf16[3,128,1536]{2,1,0:T(8,128)(2,1)S(1)}, s32[]{:S(2)}) async-start(bf16[3,192,1536]{2,1,0:T(8,128)(2,1)} %param.7), calls=%async_computation.7 | async-start | bytes 2359296 | tf_op jit(solution)/shard_map/slice | solution.py:555
  57.0 10.3 %slice-start.8 = ((bf16[3,192,1536]{2,1,0:T(8,128)(2,1)}), bf16[3,64,1536]{2,1,0:T(8,128)(2,1)S(1)}, s32[]{:S(2)}) async-start(bf16[3,192,1536]{2,1,0:T(8,128)(2,1)} %param.8), calls=%async_computation.8 | async-start | bytes 1179648 | tf_op jit(solution)/shard_map/slice | solution.py:555
  67.2 4.1 copy-start.7
  71.3 1.9 copy-start.20
  73.2 5.7 %copy-start.21 = (bf16[3,192,1536]{2,1,0:T(8,128)(2,1)S(1)}, bf16[3,192,1536]{2,1,0:T(8,128)(2,1)}, u32[]{:S(2)}) copy-start(bf16[3,192,1536]{2,1,0:T(8,128)(2,1)} %copy-done.20) | copy-start | bytes 5308420
  78.9 1.9 copy-start.11
  78.9 2.7 copy-start.9
  78.9 2.7 copy-start.23
  84.8 44.0 %copy-start.15 = (bf16[3,192,1536]{2,1,0:T(8,128)(2,1)S(1)}, bf16[3,192,1536]{2,1,0:T(8,128)(2,1)}, u32[]{:S(2)}) copy-start(bf16[3,192,1536]{2,1,0:T(8,128)(2,1)} %get-tuple-element.35) | copy-start | bytes 5308420
  128.8 3.3 copy-start.2
  132.1 2.0 copy-start.25
  178.6 5.0 %copy-start.3 = (s32[8,128,384]{2,1,0:T(8,128)S(1)}, s32[8,128,384]{2,1,0:T(8,128)}, u32[]{:S(2)}) copy-start(s32[8,128,384]{2,1,0:T(8,128)} %param.10) | copy-start | bytes 4718596
  182.4 1.2 copy-start.4
  244.9 7.9 %copy-start.5 = (f32[1024,384]{1,0:T(8,128)S(1)}, f32[1024,384]{1,0:T(8,128)}, u32[]{:S(2)}) copy-start(f32[1024,384]{1,0:T(8,128)} %copy-done.4) | copy-start | bytes 4718596
  248.0 67.8 %collective-permute-start.1 = (bf16[32,8,192]{2,1,0:T(8,128)(2,1)}, bf16[32,8,192]{2,1,0:T(8,128)(2,1)}, u32[]{:S(2)}, u32[]{:S(2)}) collective-permute-start(bf16[32,8,192]{2,1,0:T(8,128)(2,1)} %get-tuple-element.18), channel_id=1, source_target_pairs={{1,0},{2,1},{3,2},{4,3},{5,4},{6,5},{7,6},{8,7},{9,8},{10,9},{11,1... | collective-permute-start | bytes 294920 | tf_op jit(solution)/shard_map/ppermute | solution.py:528
  249.9 65.9 %collective-permute-start = (bf16[32,8,192]{2,1,0:T(8,128)(2,1)}, bf16[32,8,192]{2,1,0:T(8,128)(2,1)}, u32[]{:S(2)}, u32[]{:S(2)}) collective-permute-start(bf16[32,8,192]{2,1,0:T(8,128)(2,1)} %get-tuple-element.17), channel_id=1, source_target_pairs={{0,1},{1,2},{2,3},{3,4},{4,5},{5,6},{6,7},{7,8},{8,9},{9,10},{10,1... | collective-permute-start | bytes 294920 | tf_op jit(solution)/shard_map/ppermute | solution.py:527
  252.8 8.0 %slice-start.2 = ((s8[4718592]{0:T(1024)(128)(4,1)}), s8[4194304]{0:T(1024)(128)(4,1)S(1)}, s32[]{:S(2)}) async-start(s8[4718592]{0:T(1024)(128)(4,1)} %bitcast.226), calls=%async_computation.2 | async-start | bytes 8388608
  254.8 6.0 %slice-start.3 = ((s8[4718592]{0:T(1024)(128)(4,1)}), s8[524288]{0:T(1024)(128)(4,1)S(1)}, s32[]{:S(2)}) async-start(s8[4718592]{0:T(1024)(128)(4,1)} %bitcast.226), calls=%async_computation.3 | async-start | bytes 1048576
  260.8 1.9 copy-start.10
  260.8 2.8 copy-start.12
  263.7 6.1 %copy-start.16 = (bf16[3,192,1536]{2,1,0:T(8,128)(2,1)S(1)}, bf16[3,192,1536]{2,1,0:T(8,128)(2,1)}, u32[]{:S(2)}) copy-start(bf16[3,192,1536]{2,1,0:T(8,128)(2,1)} %get-tuple-element.35) | copy-start | bytes 5308420
  299.9 3.0 copy-start.19
  299.9 3.0 copy-start.24
  315.8 2.3 slice-start
  317.1 1.9 slice-start.1
  321.7 39.0 %copy-start.13 = (f32[1024,192]{1,0:T(8,128)S(1)}, f32[1024,192]{1,0:T(8,128)}, u32[]{:S(2)}) copy-start(f32[1024,192]{1,0:T(8,128)} %chan_scatter.2) | copy-start | bytes 2359300
  321.7 39.0 %copy-start.22 = (f32[1024,192]{1,0:T(8,128)S(1)}, f32[1024,192]{1,0:T(8,128)}, u32[]{:S(2)}) copy-start(f32[1024,192]{1,0:T(8,128)} %get-tuple-element.29) | copy-start | bytes 2359300
  360.6 2.2 copy-start.8
  362.8 2.1 copy-start.18
  366.2 4.0 slice-start.4
  369.2 1.1 slice-start.5
  373.5 37.2 %copy-start.1 = (bf16[1536,384]{1,0:T(8,128)(2,1)S(1)}, bf16[1536,384]{1,0:T(8,128)(2,1)}, u32[]{:S(2)}) copy-start(bf16[1536,384]{1,0:T(8,128)(2,1)} %param.9) | copy-start | bytes 3538948

commit v2 on v0

v2 whole, which is shorter than its diff:
```python
import functools

import jax
import jax.numpy as jnp
from jax import lax
from jax.experimental import pallas as pl
from jax.experimental.pallas import tpu as pltpu
from jax.sharding import PartitionSpec as P

DMAX = 32
NZ = 8
MESH = pl.DeviceIdType.MESH
BF = jnp.bfloat16
F32 = jnp.float32


def remote(src, dst, send, recv, device):
    return pltpu.make_async_remote_copy(
        src_ref=src, dst_ref=dst, send_sem=send, recv_sem=recv, device_id=device, device_id_type=MESH
    )


def greet(devices):
    barrier = pltpu.get_barrier_semaphore()
    for device in devices:
        pl.semaphore_signal(barrier, inc=1, device_id=device, device_id_type=MESH)
    pl.semaphore_wait(barrier, len(devices))


def z_neighbours():
    z = lax.axis_index("dp")
    return z, lax.rem(z + 1, NZ), lax.rem(z + NZ - 1, NZ)


def seq_neighbours():
    s, n = lax.axis_index("seq"), lax.axis_size("seq")
    return s, lax.rem(s + 1, n), lax.rem(s + n - 1, n)


def ring_gather(own, slot, half_rows, send_sem, recv_sem, on_block):
    z, right, left = z_neighbours()
    copies = {}
    for way in (0, 1):
        sign = -1 if way == 0 else 1
        peer = {"dp": right if way == 0 else left}
        for step in range(4):
            block = lax.rem(z + sign * step + NZ, NZ)
            for half in (0, 1):
                if step == 3 and half != way:
                    continue
                source = own(half) if step == 0 else slot(block, half)
                copies[way, step, half] = remote(
                    source, slot(block, half), send_sem.at[way, step, half], recv_sem.at[way, step, half], peer
                )
    for half in (0, 1):
        for way in (0, 1):
            copies[way, 0, half].start()
    on_block(0, z)
    for step in (1, 2, 3):
        for half in (0, 1):
            for way in (0, 1):
                copies[way, step - 1, half].wait_recv()
                if (way, step, half) in copies:
                    copies[way, step, half].start()
        on_block(2 * step - 1, lax.rem(z - step + NZ, NZ))
        on_block(2 * step, lax.rem(z + step, NZ))
    copies[0, 3, 0].wait_recv()
    copies[1, 3, 1].wait_recv()
    on_block(7, lax.rem(z + 4, NZ))
    for copy in copies.values():
        copy.wait_send()


def rows_gather_kernel(x_ref, out_ref, send_sem, recv_sem, edge_send, edge_recv, own_sem):
    length = x_ref.shape[0]
    z, right, left = z_neighbours()
    s, after, before = seq_neighbours()
    greet([{"dp": right}, {"dp": left}, {"seq": after}, {"seq": before}])
    mine = pltpu.make_async_copy(x_ref, out_ref.at[z, pl.ds(DMAX, length)], own_sem)
    mine.start()
    half_rows = length // 2
    edges = []

    def on_block(order, block):
        if order == 0:
            first, last = x_ref.at[pl.ds(0, DMAX)], x_ref.at[pl.ds(length - DMAX, DMAX)]
        else:
            first, last = out_ref.at[block, pl.ds(DMAX, DMAX)], out_ref.at[block, pl.ds(length, DMAX)]
        for side, (src, dst, peer) in enumerate(
            (
                (last, out_ref.at[block, pl.ds(0, DMAX)], after),
                (first, out_ref.at[block, pl.ds(DMAX + length, DMAX)], before),
            )
        ):
            copy = remote(src, dst, edge_send.at[side, order], edge_recv.at[side, order], {"seq": peer})
            copy.start()
            edges.append(copy)

    ring_gather(
        lambda h: x_ref.at[pl.ds(h * half_rows, half_rows)],
        lambda k, h: out_ref.at[k, pl.ds(DMAX + h * half_rows, half_rows)],
        half_rows,
        send_sem,
        recv_sem,
        on_block,
    )
    for copy in edges:
        copy.wait_recv()
        copy.wait_send()
    mine.wait()

    @pl.when(s == 0)
    def _():
        out_ref[:, 0:DMAX, :] = jnp.zeros_like(out_ref[:, 0:DMAX, :])

    @pl.when(s == lax.axis_size("seq") - 1)
    def _():
        out_ref[:, length + DMAX :, :] = jnp.zeros_like(out_ref[:, length + DMAX :, :])


def whole(n):
    return [pl.BlockSpec(memory_space=pltpu.VMEM)] * n


def rows_gather(x, collective_id):
    length, width = x.shape
    return pl.pallas_call(
        rows_gather_kernel,
        out_shape=jax.ShapeDtypeStruct((NZ, length + 2 * DMAX, width), x.dtype),
        in_specs=whole(1),
        out_specs=whole(1)[0],
        scratch_shapes=[
            pltpu.SemaphoreType.DMA((2, 4, 2)),
            pltpu.SemaphoreType.DMA((2, 4, 2)),
            pltpu.SemaphoreType.DMA((2, 8)),
            pltpu.SemaphoreType.DMA((2, 8)),
            pltpu.SemaphoreType.DMA,
        ],
        compiler_params=pltpu.CompilerParams(collective_id=collective_id, has_side_effects=True),
        name="rows_gather",
    )(x)


LO, HI = slice(0, 64), slice(64, 128)
ROWS, PART, RIM = 1024, 512, 8 * DMAX
HALF = (ROWS + PART) // 2
CUBE = 0.044715
SLOPE = 0.7978845608028654


def activate_slope(value):
    square = value * value
    turn = jnp.tanh(SLOPE * (value + CUBE * value * square))
    return 0.5 * (1.0 + turn) + 0.5 * value * (1.0 - turn * turn) * (SLOPE * (1.0 + 3.0 * CUBE * square))


def greet_later(devices):
    barrier = pltpu.get_barrier_semaphore()
    for device in devices:
        pl.semaphore_signal(barrier, inc=1, device_id=device, device_id_type=MESH)
    return lambda: pl.semaphore_wait(barrier, len(devices))


def chunk(i, size):
    return pl.ds(pl.multiple_of(i * size, size), size)


def conv_chunk(framed, weight, spacing, index):
    total = None
    for tap in range(3):
        rows = framed[pl.ds(DMAX + (tap - 1) * spacing + 32 * index, 32)].reshape(256, 192 * NZ)
        term = lax.dot_general(rows, weight[tap], (((1,), (1,)), ((), ())), preferred_element_type=F32)
        total = term if total is None else total + term
    return total


def layer(framed, weight, spacing, base, pre_ref, hid_ref, held, z):
    @pl.loop(0, 2)
    def _(i):
        rests = []
        for index in (i, i + 2):
            pre = conv_chunk(framed, weight, spacing, index)
            hidden = (base(index).astype(F32) + jax.nn.gelu(pre)).astype(BF)
            pre_ref[chunk(index, 256), :] = pre
            if hid_ref is not None:
                hid_ref[chunk(index, 256), :] = hidden
            held[z, chunk(index, 256), :] = hidden[:, 0:128]
            rests.append(hidden[:, 128:192])
        held[z, pl.ds(pl.multiple_of(ROWS + 256 * i, 256), 256), :] = jnp.concatenate(rests, axis=1)


def ring_held(held, send_sem, recv_sem, on_block):
    z = lax.axis_index("dp")
    ring_gather(
        lambda h: held.at[z, pl.ds(h * HALF, HALF)],
        lambda k, h: held.at[k, pl.ds(h * HALF, HALF)],
        HALF,
        send_sem,
        recv_sem,
        on_block,
    )


def unpack(held, out_ref, base):
    for j in range(NZ // 2):
        one, two, lane = 2 * j, 2 * j + 1, 384 * j
        out_ref[base : base + ROWS, lane : lane + 128] = held[one, 0:ROWS, :]
        out_ref[base : base + ROWS, lane + 256 : lane + 384] = held[two, 0:ROWS, :]
        for h, lanes in ((0, LO), (1, HI)):
            out_ref[base + h * PART : base + (h + 1) * PART, lane + 128 : lane + 256] = jnp.concatenate(
                [held[one, ROWS : ROWS + PART, lanes], held[two, ROWS : ROWS + PART, lanes]], axis=1
            )


def first_kernel(
    gaps, fe_ref, w_ref, pre_ref, hid_ref, out_ref, held, edge, send_sem, recv_sem, edge_send, edge_recv
):
    z, right, left = z_neighbours()
    s, after, before = seq_neighbours()
    met = greet_later([{"dp": right}, {"dp": left}, {"seq": after}, {"seq": before}])
    odd = lax.rem(z, 2) == 1

    def base(index):
        rows = pl.ds(DMAX + 32 * index, 32)
        main = fe_ref[rows, :, pl.ds(pl.multiple_of(128 * (3 * (z // 2) + 2 * lax.rem(z, 2)), 128), 128)].reshape(256, 128)
        rest = fe_ref[rows, :, pl.ds(pl.multiple_of(128 * (3 * (z // 2) + 1), 128), 128)].reshape(256, 128)
        rest = jnp.where(odd, rest[:, HI].astype(F32), rest[:, LO].astype(F32))
        return jnp.concatenate([main.astype(F32), rest], axis=1)

    layer(fe_ref, w_ref, gaps[0], base, pre_ref, hid_ref, held, z)
    met()
    edges = []

    def on_block(order, block):
        for side, piece, at, peer in (
            (0, 0, ROWS - RIM, after),
            (0, 1, ROWS + PART - RIM, after),
            (1, 0, 0, before),
            (1, 1, ROWS, before),
        ):
            copy = remote(
                held.at[block, pl.ds(at, RIM)],
                edge.at[side, block, pl.ds(piece * RIM, RIM)],
                edge_send.at[side, piece, order],
                edge_recv.at[side, piece, order],
                {"seq": peer},
            )
            copy.start()
            edges.append(copy)

    ring_held(held, send_sem, recv_sem, on_block)
    unpack(held, out_ref, RIM)
    for copy in edges:
        copy.wait_recv()
        copy.wait_send()
    n = lax.axis_size("seq")
    for side, at, lanes, keep in ((0, 0, HI, s > 0), (1, RIM + ROWS, LO, s < n - 1)):
        for j in range(NZ // 2):
            one, two, lane = 2 * j, 2 * j + 1, 384 * j
            pieces = (
                edge[side, one, 0:RIM, :],
                jnp.concatenate([edge[side, one, RIM : 2 * RIM, lanes], edge[side, two, RIM : 2 * RIM, lanes]], axis=1),
                edge[side, two, 0:RIM, :],
            )
            for i, piece in enumerate(pieces):
                out_ref[at : at + RIM, lane + 128 * i : lane + 128 * (i + 1)] = jnp.where(
                    keep, piece, jnp.zeros_like(piece)
                )


SMEM = pl.BlockSpec(memory_space=pltpu.SMEM)


def call(kernel, name, collective_id, out_shapes, in_specs, scratch, *operands):
    return pl.pallas_call(
        kernel,
        out_shape=tuple(jax.ShapeDtypeStruct(*o) for o in out_shapes),
        in_specs=in_specs,
        out_specs=tuple(whole(len(out_shapes))),
        scratch_shapes=scratch,
        compiler_params=pltpu.CompilerParams(collective_id=collective_id, has_side_effects=True),
        name=name,
    )(*operands)


DMA = pltpu.SemaphoreType.DMA
PACKED = (ROWS + PART, 128)


def first_layer(gaps, framed_in, weight):
    return call(
        first_kernel,
        "first_layer",
        1,
        [((ROWS, 192), F32), ((ROWS, 192), BF), ((ROWS + 2 * RIM, 192 * NZ), BF)],
        [SMEM] + whole(2),
        [
            pltpu.VMEM((NZ, *PACKED), BF),
            pltpu.VMEM((2, NZ, 2 * RIM, 128), BF),
            DMA((2, 4, 2)),
            DMA((2, 4, 2)),
            DMA((2, 2, 8)),
            DMA((2, 2, 8)),
        ],
        gaps,
        framed_in,
        weight,
    )


def seq_place():
    s = lax.axis_index("seq")
    return s // 8, lax.rem(s // 2, 4), lax.rem(s, 2)


def seq_peers():
    y, x, core = seq_place()
    at = lambda y, x, core: (y * 4 + x) * 2 + core
    other = at(y, x, 1 - core)
    along_x = [at(y, lax.rem(x + d, 4), core) for d in (1, 2, 3)]
    along_y = [at(lax.rem(y + d, 4), x, core) for d in (1, 2, 3)]
    return other, along_x, along_y


def merge_stats(stats, merged, got, send_sem, recv_sem, own_sem):
    y, x, core = seq_place()
    other, along_x, along_y = seq_peers()
    stages = ((2, core, [other]), (4, x, along_x), (4, y, along_y))
    for number, (count, place, peers) in enumerate(stages):
        source = stats if number == 0 else merged.at[number - 1]
        copies = []
        for d, peer in enumerate(peers):
            copy = remote(
                source, got.at[number, place], send_sem.at[number, d], recv_sem.at[number, d], {"seq": peer}
            )
            copy.start()
            copies.append(copy)
        mine = pltpu.make_async_copy(source, got.at[number, place], own_sem.at[number])
        mine.start()
        mine.wait()
        for copy in copies:
            copy.wait_recv()
        peak = got[number, 0, 0]
        for i in range(1, count):
            peak = jnp.maximum(peak, got[number, i, 0])
        sums = [jnp.zeros_like(peak) for _ in range(3)]
        for i in range(count):
            sums[0] = sums[0] + got[number, i, 1] * jnp.exp(got[number, i, 0] - peak)
            sums[1] = sums[1] + got[number, i, 2]
            sums[2] = sums[2] + got[number, i, 3]
        for copy in copies:
            copy.wait_send()
        if number < 2:
            merged[number, 0] = peak
            for i in range(3):
                merged[number, i + 1] = sums[i]
    return peak, *sums


def second_kernel(
    gaps,
    f_ref,
    w_ref,
    hid_ref,
    head_ref,
    counts_ref,
    pre_ref,
    out_ref,
    grad_ref,
    loss_ref,
    held,
    logits,
    targets,
    stats,
    merged,
    got,
    send_sem,
    recv_sem,
    stat_send,
    stat_recv,
    stat_own,
):
    z, right, left = z_neighbours()
    other, along_x, along_y = seq_peers()
    met = greet_later([{"dp": right}, {"dp": left}] + [{"seq": p} for p in [other, *along_x, *along_y]])
    layer(f_ref, w_ref, gaps[1], lambda index: hid_ref[chunk(index, 256), :], pre_ref, None, held, z)
    met()

    def on_block(order, block):
        if order in (1, 3):

            @pl.loop(4 * (order - 1), 4 * (order + 1))
            def _(i):
                targets[chunk(i, 8)] = jnp.swapaxes(counts_ref[:, chunk(i, 8), :], 0, 1).astype(F32)

    ring_held(held, send_sem, recv_sem, on_block)
    unpack(held, out_ref, 0)
    shape = stats.shape[1:]

    def forward(i, carry):
        peak, count, cross = carry
        value = jnp.dot(out_ref[chunk(i, 256), :], head_ref[...], preferred_element_type=F32).reshape(32, *shape)
        logits[chunk(i, 32)] = value
        target = targets[chunk(i, 32)]
        return (
            jnp.maximum(peak, jnp.max(value, axis=0)),
            count + jnp.sum(target, axis=0),
            cross + jnp.sum(target * value, axis=0),
        )

    zero = jnp.zeros(shape, F32)
    peak, count, cross = lax.fori_loop(0, 4, forward, (jnp.full(shape, -jnp.inf, F32), zero, zero))
    spread = lax.fori_loop(
        0, 8, lambda i, t: t + jnp.sum(jnp.exp(logits[chunk(i, 16)] - peak[None]), axis=0), zero
    )
    for i, value in enumerate((peak, spread, count, cross)):
        stats[i] = value
    peak, spread, count, cross = merge_stats(stats, merged, got, stat_send, stat_recv, stat_own)
    lse = peak + jnp.log(spread)
    bins = 128 * lax.axis_size("seq")
    loss_ref[...] = (count * lse - cross) / bins

    @pl.loop(0, 8)
    def _(i):
        value = (count[None] * jnp.exp(logits[chunk(i, 16)] - lse[None]) - targets[chunk(i, 16)]) * (1.0 / bins)
        grad_ref[chunk(i, 128), :] = value.reshape(128, shape[1]).astype(BF)


def second_layer(gaps, framed_one, weight, hidden_one, head_weight, counts):
    tracks = head_weight.shape[1]
    stat = (4, NZ, tracks)
    return call(
        second_kernel,
        "second_layer",
        2,
        [((ROWS, 192), F32), ((ROWS, 192 * NZ), BF), ((ROWS, tracks), BF), ((NZ, tracks), F32)],
        [SMEM] + whole(5),
        [
            pltpu.VMEM((NZ, *PACKED), BF),
            pltpu.VMEM((128, NZ, tracks), F32),
            pltpu.VMEM((128, NZ, tracks), F32),
            pltpu.VMEM(stat, F32),
            pltpu.VMEM((2, *stat), F32),
            pltpu.VMEM((3, 4, *stat), F32),
            DMA((2, 4, 2)),
            DMA((2, 4, 2)),
            DMA((3, 3)),
            DMA((3, 3)),
            DMA((3,)),
        ],
        gaps,
        framed_one,
        weight,
        hidden_one,
        head_weight,
        counts,
    )


def ring_scatter(own, got, sent, send_sem, recv_sem, pair_of, hook):
    z, right, left = z_neighbours()
    piece = lambda h: pl.ds(h * HALF, HALF)
    far = lax.rem(z + 4, NZ) // 2
    pair_of(far)
    copies = {}
    for step in range(4):
        for half in (0, 1):
            for way in (0, 1):
                if step == 0 and half != way:
                    continue
                sign = 1 if way == 0 else -1
                block = lax.rem(z + sign * (4 - step) + NZ, NZ)
                before = copies.get((way, step - 1, half))
                if before is None:
                    source = own.at[block, piece(half)]
                else:
                    before.wait_recv()
                    sent[way, step - 1, piece(half), :] = (
                        got[way, step - 1, piece(half), :].astype(F32) + own[block, piece(half), :].astype(F32)
                    ).astype(BF)
                    source = sent.at[way, step - 1, piece(half)]
                copy = remote(
                    source,
                    got.at[way, step, piece(half)],
                    send_sem.at[way, step, half],
                    recv_sem.at[way, step, half],
                    {"dp": right if way == 0 else left},
                )
                copy.start()
                copies[way, step, half] = copy
        if step == 0:
            for d in (1, 3, 2):
                pair_of(lax.rem(far + d, NZ // 2))
        hook(step)
    for half in (0, 1):
        copies[0, 3, half].wait_recv()
        copies[1, 3, half].wait_recv()
    for copy in copies.values():
        copy.wait_send()


def ring_total(own, got, at, size):
    z = lax.axis_index("dp")
    rows = pl.ds(pl.multiple_of(at, 256), size)
    return own[z, rows, :].astype(F32) + got[0, 3, rows, :].astype(F32) + got[1, 3, rows, :].astype(F32)


def ring_result(own, got, i):
    rest = ring_total(own, got, ROWS + 256 * i, 256)
    return [
        (index, jnp.concatenate([ring_total(own, got, 256 * index, 256), rest[:, lanes]], axis=1))
        for index, lanes in ((i, LO), (i + 2, HI))
    ]


def put_pair(own, pair, i, product):
    one, two = 2 * pair, 2 * pair + 1
    for index, value in zip((i, i + 2), product):
        own[one, chunk(index, 256), :] = value[:, 0:128]
        own[two, chunk(index, 256), :] = value[:, 256:384]
    rows = pl.ds(pl.multiple_of(ROWS + 256 * i, 256), 256)
    low, high = product
    own[one, rows, :] = jnp.concatenate([low[:, 128:192], high[:, 128:192]], axis=1)
    own[two, rows, :] = jnp.concatenate([low[:, 192:256], high[:, 192:256]], axis=1)


class Spread:
    def __init__(self, source, result, first, number, scratch):
        self.source, self.result, self.first, self.number = source, result, first, number
        self.pair, self.both, self.got_one, self.mid, self.got_two, self.send, self.recv = scratch
        self.y, self.x, self.core = seq_place()
        self.other, self.along_x, self.along_y = seq_peers()

    def stage(self, which):
        along = self.first if which == 1 else ("y" if self.first == "x" else "x")
        return (self.x, self.along_x) if along == "x" else (self.y, self.along_y)

    def copy(self, source, target, slot, peer):
        made = remote(source, target, self.send.at[self.number, slot], self.recv.at[self.number, slot], {"seq": peer})
        made.start()
        return made

    def begin(self):
        self.exchange = self.copy(self.source(1 - self.core), self.pair, 0, self.other)

    def add_pair(self):
        self.exchange.wait_recv()
        mine = self.source(self.core)

        @pl.loop(0, 16)
        def _(i):
            spot = lax.rem(i, 4) * 4 + i // 4 if self.first == "x" else i
            self.both[spot] = (self.pair[i].astype(F32) + mine[i].astype(F32)).astype(BF)

        place, peers = self.stage(1)
        self.copies = []
        for d, peer in enumerate(peers):
            target = lax.rem(place + d + 1, 4)
            self.copies.append(self.copy(self.both.at[pl.ds(4 * target, 4)], self.got_one.at[2 - d], 1 + d, peer))

    def add_first(self):
        for copy in self.copies:
            copy.wait_recv()
        place, _ = self.stage(1)

        @pl.loop(0, 4)
        def _(i):
            total = self.both[4 * place + i].astype(F32)
            for d in range(3):
                total = total + self.got_one[d, i].astype(F32)
            self.mid[i] = total.astype(BF)

        place, peers = self.stage(2)
        self.later = []
        for d, peer in enumerate(peers):
            target = lax.rem(place + d + 1, 4)
            self.later.append(self.copy(self.mid.at[target], self.got_two.at[2 - d], 4 + d, peer))

    def finish(self):
        for copy in self.later:
            copy.wait_recv()
        place, _ = self.stage(2)
        total = self.mid[place].astype(F32)
        for d in range(3):
            total = total + self.got_two[d].astype(F32)
        self.result[...] = total
        for copy in [self.exchange, *self.copies, *self.later]:
            copy.wait_send()


def spread_scratch(rows, width):
    return [
        pltpu.VMEM((16, rows, width), BF),
        pltpu.VMEM((16, rows, width), BF),
        pltpu.VMEM((3, 4, rows, width), BF),
        pltpu.VMEM((4, rows, width), BF),
        pltpu.VMEM((3, rows, width), BF),
    ]


def ring_scratch():
    return [
        pltpu.VMEM((NZ, *PACKED), BF),
        pltpu.VMEM((2, 4, *PACKED), BF),
        pltpu.VMEM((2, 3, *PACKED), BF),
        DMA((2, 4, 2)),
        DMA((2, 4, 2)),
    ]


def seq_hellos():
    other, along_x, along_y = seq_peers()
    return [other, *along_x, *along_y]


def third_kernel(
    grad_ref,
    head_ref,
    rows_ref,
    pre_ref,
    back_ref,
    up_ref,
    head_out,
    own,
    got,
    sent,
    send_sem,
    recv_sem,
    head_grad,
    pair,
    both,
    got_one,
    mid,
    got_two,
    spread_send,
    spread_recv,
    edge_send,
    edge_recv,
):
    z, right, left = z_neighbours()
    s, after, before = seq_neighbours()
    met = greet_later(
        [{"dp": right}, {"dp": left}, {"seq": after}, {"seq": before}] + [{"seq": p} for p in seq_hellos()]
    )
    started = []

    def pair_of(p):
        @pl.loop(0, 2)
        def _(i):
            product = [
                lax.dot_general(
                    grad_ref[chunk(index, 256), :],
                    head_ref[chunk(p, 384), :],
                    (((1,), (1,)), ((), ())),
                    preferred_element_type=F32,
                ).astype(BF)
                for index in (i, i + 2)
            ]
            put_pair(own, p, i, product)

        if not started:
            met()
            started.append(1)

    scratch = (pair, both, got_one, mid, got_two, spread_send, spread_recv)
    spread = Spread(lambda core: head_grad.at[:, core], head_out, "x", 0, scratch)

    def hook(step):
        if step == 0:

            @pl.loop(0, 4)
            def _(c):
                value = lax.dot_general(
                    rows_ref[:, chunk(c, 384)], grad_ref[...], (((0,), (0,)), ((), ())), preferred_element_type=F32
                )
                head_grad[chunk(c, 4)] = value.astype(BF).reshape(4, 2, 48, value.shape[1])

            spread.begin()
        elif step == 1:
            spread.add_pair()
        elif step == 2:
            spread.add_first()
        else:
            spread.finish()

    ring_scatter(own, got, sent, send_sem, recv_sem, pair_of, hook)

    @pl.loop(0, 2)
    def _(i):
        for index, value in ring_result(own, got, i):
            back_ref[chunk(index, 256), :] = value
            up = (value * activate_slope(pre_ref[chunk(index, 256), :])).astype(BF)
            up_ref[pl.ds(DMAX + 32 * index, 32)] = up.reshape(32, NZ, 192)

    edges = []
    for side, (src, dst, peer) in enumerate(((128, 0, after), (DMAX, DMAX + 128, before))):
        copy = remote(
            up_ref.at[pl.ds(src, DMAX)], up_ref.at[pl.ds(dst, DMAX)], edge_send.at[side], edge_recv.at[side], {"seq": peer}
        )
        copy.start()
        edges.append(copy)
    for copy in edges:
        copy.wait_recv()
        copy.wait_send()
    for at, drop in ((0, s == 0), (DMAX + 128, s == lax.axis_size("seq") - 1)):

        @pl.when(drop)
        def _():
            up_ref[at : at + DMAX] = jnp.zeros_like(up_ref[at : at + DMAX])


def third_layer(logit_grad, head_weight, head_rows, pre_two):
    tracks = head_weight.shape[1]
    return call(
        third_kernel,
        "third_layer",
        3,
        [((ROWS, 192), F32), ((128 + 2 * DMAX, NZ, 192), BF), ((48, tracks), F32)],
        whole(4),
        ring_scratch()
        + [pltpu.VMEM((16, 2, 48, tracks), BF)]
        + spread_scratch(48, tracks)
        + [DMA((1, 7)), DMA((1, 7)), DMA((2,)), DMA((2,))],
        logit_grad,
        head_weight,
        head_rows,
        pre_two,
    )


def tap_grad(framed, spacing, up, tap, into):
    @pl.loop(0, 4)
    def _(c):
        rows = framed[pl.ds(DMAX + (tap - 1) * spacing, 128), :, chunk(c, 384)].reshape(ROWS, 384)
        value = lax.dot_general(rows, up, (((0,), (0,)), ((), ())), preferred_element_type=F32)
        into[chunk(c, 4)] = value.astype(BF).reshape(4, 2, 48, 192)


def fourth_kernel(
    gaps,
    up_ref,
    w_ref,
    back_ref,
    pre_ref,
    f_ref,
    one_ref,
    two_out,
    own,
    got,
    sent,
    send_sem,
    recv_sem,
    grads,
    pair,
    both,
    got_one,
    mid,
    got_two,
    spread_send,
    spread_recv,
):
    z, right, left = z_neighbours()
    met = greet_later([{"dp": right}, {"dp": left}] + [{"seq": p} for p in seq_hellos()])
    gap = gaps[1]
    started = []

    def pair_of(p):
        @pl.loop(0, 2)
        def _(i):
            product = []
            for index in (i, i + 2):
                total = None
                for tap in range(3):
                    rows = up_ref[pl.ds(DMAX - (tap - 1) * gap + 32 * index, 32)].reshape(256, 192)
                    term = jnp.dot(rows, w_ref[tap, :, chunk(p, 384)], preferred_element_type=F32)
                    total = term if total is None else total + term
                product.append(total.astype(BF))
            put_pair(own, p, i, product)

        if not started:
            met()
            started.append(1)

    spreads = [
        Spread(
            lambda core, t=t: grads.at[t, :, core],
            two_out.at[t],
            "xyx"[t],
            t,
            tuple(r.at[t] for r in (pair, both, got_one, mid, got_two)) + (spread_send, spread_recv),
        )
        for t in range(3)
    ]

    def hook(step):
        up = lambda: up_ref[DMAX : DMAX + 128].reshape(ROWS, 192)
        if step == 0:
            tap_grad(f_ref, gap, up(), 0, grads.at[0])
            spreads[0].begin()
        elif step == 1:
            tap_grad(f_ref, gap, up(), 1, grads.at[1])
            spreads[1].begin()
            tap_grad(f_ref, gap, up(), 2, grads.at[2])
            spreads[2].begin()
        elif step == 2:
            for t in range(3):
                spreads[t].add_pair()
        else:
            for t in range(3):
                spreads[t].add_first()

    ring_scatter(own, got, sent, send_sem, recv_sem, pair_of, hook)

    @pl.loop(0, 2)
    def _(i):
        for index, value in ring_result(own, got, i):
            rows = chunk(index, 256)
            one_ref[rows, :] = ((back_ref[rows, :] + value) * activate_slope(pre_ref[rows, :])).astype(BF)

    for t in range(3):
        spreads[t].finish()


def fourth_layer(gaps, framed_up, weight, back, pre_one, framed_one):
    taps = lambda shapes: [pltpu.VMEM((3, *s.shape), s.dtype) for s in shapes]
    return call(
        fourth_kernel,
        "fourth_layer",
        4,
        [((ROWS, 192), BF), ((3, 48, 192), F32)],
        [SMEM] + whole(5),
        ring_scratch()
        + [pltpu.VMEM((3, 16, 2, 48, 192), BF)]
        + taps(spread_scratch(48, 192))
        + [DMA((3, 7)), DMA((3, 7))],
        gaps,
        framed_up,
        weight,
        back,
        pre_one,
        framed_one,
    )


def fifth_kernel(
    gaps, fe_ref, up_ref, one_out, grads, pair, both, got_one, mid, got_two, spread_send, spread_recv
):
    met = greet_later([{"seq": p} for p in seq_hellos()])
    spreads = [
        Spread(
            lambda core, t=t: grads.at[t, :, core],
            one_out.at[t],
            "xyx"[t],
            t,
            tuple(r.at[t] for r in (pair, both, got_one, mid, got_two)) + (spread_send, spread_recv),
        )
        for t in range(3)
    ]
    for t in range(3):
        tap_grad(fe_ref, gaps[0], up_ref[...], t, grads.at[t])
        if t == 0:
            met()
        spreads[t].begin()
    for t in range(3):
        spreads[t].add_pair()
    for t in range(3):
        spreads[t].add_first()
    for t in range(3):
        spreads[t].finish()


def fifth_layer(gaps, framed_in, up_one):
    taps = lambda shapes: [pltpu.VMEM((3, *s.shape), s.dtype) for s in shapes]
    return call(
        fifth_kernel,
        "fifth_layer",
        5,
        [((3, 48, 192), F32)],
        [SMEM] + whole(2),
        [pltpu.VMEM((3, 16, 2, 48, 192), BF)] + taps(spread_scratch(48, 192)) + [DMA((3, 7)), DMA((3, 7))],
        gaps,
        framed_in,
        up_one,
    )[0]


def on_device(embeddings, conv_one, conv_two, head_weight, counts, dilation):
    odd = lax.rem(lax.axis_index("dp"), 2) == 1
    turn = lambda w: jnp.where(odd, jnp.concatenate([w[:, 64:], w[:, :64]], axis=1), w)
    back_turn = lambda g: jnp.where(odd, jnp.concatenate([g[..., 128:], g[..., :128]], axis=-1), g)
    w_one, w_two = turn(conv_one), turn(conv_two)
    framed_in = jnp.transpose(rows_gather(embeddings[0], 0), (1, 0, 2))
    pre_one, hidden_one, framed_one = first_layer(dilation, framed_in, w_one)
    framed_one = framed_one.reshape(framed_in.shape)
    pre_two, head_rows, logit_grad, track_loss = second_layer(
        dilation, framed_one, w_two, hidden_one, head_weight, counts
    )
    grad_two_out, framed_up, grad_head = third_layer(logit_grad, head_weight, head_rows, pre_two)
    up_one, grad_two = fourth_layer(dilation, framed_up, w_two, grad_two_out, pre_one, framed_one)
    grad_one = fifth_layer(dilation, framed_in, up_one)
    return (track_loss, grad_head, back_turn(grad_one), back_turn(grad_two))


def solution(mesh):
    placed = (
        P("dp", "seq", None),
        P(None, "dp", None),
        P(None, "dp", None),
        P(None, "dp"),
        P(None, "seq", "dp"),
        P(),
    )
    return jax.shard_map(
        on_device,
        mesh=mesh,
        in_specs=placed,
        out_specs=(P(None, "dp"), P("seq", "dp"), P(None, "seq", "dp"), P(None, "seq", "dp")),
        check_vma=False,
    )
```

time: 856 us -> 284 us (0.33)
  waiting for transfers between devices: 461 us -> 0 us
  Pallas kernels: 0 us -> 264 us
  blocking collectives: 246 us -> 0 us
  matrix products: 43.2 us -> 0 us
  local copies, waits for them, and re-layouts: 53.6 us -> 13.2 us
  between operations: 19.1 us -> 0.77 us
  starting transfers between devices: 17.7 us -> 0 us
  other arithmetic: 13.6 us -> 4.78 us
    pallas_call x0 -> x6, Pallas kernels: none -> 264 us  [the longest x5 220 us: call(): pl.pallas_call(kernel, out_shape=tuple((jax.ShapeDtypeStruct(*o) for o in...]
    reduce_scatter x3 -> x0, waiting for transfers between devices: 168 us -> none  [the longest x1 88.5 us: on_device(): lax.psum_scatter(jnp.einsum('blc,blt->ct', head_rows, logit_grad, preferr...]
    all_gather x3 -> x0, waiting for transfers between devices: 143 us -> none  [the longest x1 49.8 us: framed_input(): gathered = lax.all_gather(block, 'dp', axis=0, tiled=True)]
    unnamed x8 -> x0, waiting for transfers between devices: 136 us -> none
    psum x1 -> x0, blocking collectives: 124 us -> none  [on_device(): lax.psum((exp_local, count_local, cross_local), 'seq')]
    pmax x1 -> x0, blocking collectives: 122 us -> none  [on_device(): peak_all = lax.pmax(local_peak, 'seq')]
    dot_general x18 -> x0, matrix products: 43.2 us -> none  [the longest x6 13.9 us: weight_grad(): jnp.einsum('blc,bld->cd', tap_rows, upstream, preferred_element_type=jnp....]
    convert_element_type x4 -> x0, local copies, waits for them, and re-layouts: 22.2 us -> none  [the longest x1 10.1 us: on_device(): back_partial.astype(jnp.bfloat16)]
  transfers between devices with their start and end apart: 13 -> 0, of which waited for: 12 -> 0; matrix products, arithmetic and copies ran while one was open for 4% -> 0% of each run, Pallas kernels for 0% -> 0%
where the time goes in v2:
time: 284 us; the launch traced here: 283 us
  Pallas kernels  264 us (93%)
  local copies, waits for them, and re-layouts  13.2 us (5%)
  other arithmetic  4.78 us (2%)
    pallas_call x5, Pallas kernels, call(): pl.pallas_call(kernel, out_shape=tuple((jax.ShapeDtypeStruct(*o) for o in...  220 us
    pallas_call x1, Pallas kernels, rows_gather(): pl.pallas_call(rows_gather_kernel, out_shape=jax.ShapeDtypeStruct((NZ, le...  44.5 us
    pallas_call x1, local copies, waits for them, and re-layouts, rows_gather(): pl.pallas_call(rows_gather_kernel, out_shape=jax.ShapeDtypeStruct((NZ, le...  7.05 us

profile of v2, /device:TPU:2, one launch (start us, length us, event | category | flops | bytes accessed | tf_op | source)
XLA Modules:
  0.0 282.7 jit_solution(5151765963466732030)
XLA Ops:
  0.6 0.0 copy-start.1
  0.6 0.0 slice-start.3
  0.7 0.0 copy-start
  0.7 0.0 slice-start
  0.7 0.0 slice-start.1
  0.7 0.0 slice-start.2
  0.7 1.4 copy-done.1
  2.1 0.5 slice-done.3
  2.6 0.4 copy-done
  3.0 0.2 slice-done
  3.2 0.4 slice-done.1
  3.6 0.2 slice-done.2
  3.8 2.3 maximum_select_fusion
  6.1 44.5 %rows_gather.1 = bf16[8,192,1536]{2,1,0:T(8,128)(2,1)} custom-call(bf16[128,1536]{1,0:T(8,128)(2,1)} %bitcast.9), custom_call_target="tpu_custom_call" | custom-call | tf_op jit(solution)/shard_map/rows_gather/pallas_call | solution.py:127
  50.6 7.0 %copy.12 = bf16[8,192,1536]{2,0,1:T(8,128)(2,1)} copy(bf16[8,192,1536]{2,1,0:T(8,128)(2,1)} %rows_gather.1) | data formatting | bytes 9437184 | tf_op jit(solution)/shard_map/rows_gather/pallas_call | solution.py:127
  57.6 47.5 %first_layer.1 = (f32[1024,192]{1,0:T(8,128)}, bf16[1024,192]{1,0:T(8,128)(2,1)}, bf16[1536,1536]{1,0:T(8,128)(2,1)}) custom-call(s32[2]{0:T(128)} %gaps.7, bf16[192,8,1536]{2,1,0:T(8,128)(2,1)} %bitcast.5, bf16[3,192,1536]{2,1,0:T(8,128)(2,1)} %get-tuple-element.28.w_ref), custom_call_target="tpu_custom_call" | custom-call | tf_op jit(solution)/shard_map/first_layer/pallas_call | solution.py:275
  105.2 59.6 %second_layer.1 = (f32[1024,192]{1,0:T(8,128)}, bf16[1024,1536]{1,0:T(8,128)(2,1)}, bf16[1024,384]{1,0:T(8,128)(2,1)}, f32[8,384]{1,0:T(8,128)}) custom-call(s32[2]{0:T(128)} %gaps.7, bf16[192,8,1536]{2,1,0:T(8,128)(2,1)} %bitcast.7, bf16[3,192,1536]{2,1,0:T(8,128)(2,1)} %get-tuple-element.29.w_ref, bf16[1024,192]{1,0:T(8,128)(2,1)} %get-tuple-element.17.hid_ref, ...), custom_call_target="tpu_custom_call" | custom-call | tf_op jit(solution)/shard_map/second_layer/pallas_call | solution.py:275
  164.8 45.0 %third_layer.1 = (f32[1024,192]{1,0:T(8,128)}, bf16[192,8,192]{2,1,0:T(8,128)(2,1)}, f32[48,384]{1,0:T(8,128)}) custom-call(bf16[1024,384]{1,0:T(8,128)(2,1)} %get-tuple-element.19.grad_ref, bf16[1536,384]{1,0:T(8,128)(2,1)} %head_ref.3, bf16[1024,1536]{1,0:T(8,128)(2,1)} %get-tuple-element.20.rows_ref, f32[1024,192]{1,0:T(8,128)} %get-tuple-element.21.pre_ref), custom_call_target="tpu_custom_call" | custom-call | tf_op jit(solution)/shard_map/third_layer/pallas_call | solution.py:275
  209.7 43.3 %fourth_layer.1 = (bf16[1024,192]{1,0:T(8,128)(2,1)}, f32[3,48,192]{2,1,0:T(8,128)}) custom-call(s32[2]{0:T(128)} %gaps.7, bf16[192,8,192]{2,1,0:T(8,128)(2,1)} %get-tuple-element.23.up_ref, bf16[3,192,1536]{2,1,0:T(8,128)(2,1)} %get-tuple-element.29.w_ref, f32[1024,192]{1,0:T(8,128)} %get-tuple-element.24.back_ref, f32[1024,192]{1,0:T(8,128)} %get-tuple-element.25.pre_ref, ...), custom_call_target="tpu_custom_call" | custom-call | tf_op jit(solution)/shard_map/fourth_layer/pallas_call | solution.py:275
  253.1 0.0 copy-start.2
  253.1 0.0 copy-start.4
  253.1 0.0 copy-start.3
  253.1 24.1 %fifth_layer.1 = f32[3,48,192]{2,1,0:T(8,128)} custom-call(s32[2]{0:T(128)} %gaps.7, bf16[192,8,1536]{2,1,0:T(8,128)(2,1)} %bitcast.6, bf16[1024,192]{1,0:T(8,128)(2,1)} %get-tuple-element.26.up_ref), custom_call_target="tpu_custom_call" | custom-call | tf_op jit(solution)/shard_map/fifth_layer/pallas_call | solution.py:275
  277.2 0.9 slice.29
  278.1 0.9 slice.28
  279.0 1.7 maximum_select_fusion.2
  280.7 0.0 copy-done.2
  280.7 0.8 maximum_select_fusion.3
  281.5 0.0 copy-done.4
  281.5 0.6 copy.15
  282.1 0.0 copy-done.3
  282.1 0.6 copy.16
  (2 shorter events, 0.0 us)
Async XLA Ops:
  0.6 1.5 copy-start.1
  0.6 2.0 slice-start.3
  0.7 2.4 copy-start
  0.7 2.5 slice-start
  0.7 2.9 %slice-start.1 = ((bf16[3,192,1536]{2,1,0:T(8,128)(2,1)}), bf16[3,128,1536]{2,1,0:T(8,128)(2,1)S(1)}, s32[]{:S(2)}) async-start(bf16[3,192,1536]{2,1,0:T(8,128)(2,1)} %param.7), calls=%async_computation.1 | async-start | bytes 2359296 | tf_op jit(solution)/shard_map/slice | solution.py:889
  0.7 3.1 %slice-start.2 = ((bf16[3,192,1536]{2,1,0:T(8,128)(2,1)}), bf16[3,64,1536]{2,1,0:T(8,128)(2,1)S(1)}, s32[]{:S(2)}) async-start(bf16[3,192,1536]{2,1,0:T(8,128)(2,1)} %param.8), calls=%async_computation.2 | async-start | bytes 1179648 | tf_op jit(solution)/shard_map/slice | solution.py:889
  253.1 27.6 %copy-start.2 = (f32[3,48,192]{2,1,0:T(8,128)S(1)}, f32[3,48,192]{2,1,0:T(8,128)}, u32[]{:S(2)}) copy-start(f32[3,48,192]{2,1,0:T(8,128)} %get-tuple-element.27) | copy-start | bytes 331780
  253.1 28.4 %copy-start.4 = (f32[8,384]{1,0:T(8,128)S(1)}, f32[8,384]{1,0:T(8,128)}, u32[]{:S(2)}) copy-start(f32[8,384]{1,0:T(8,128)} %get-tuple-element.34) | copy-start | bytes 36868
  253.1 29.0 %copy-start.3 = (f32[48,384]{1,0:T(8,128)S(1)}, f32[48,384]{1,0:T(8,128)}, u32[]{:S(2)}) copy-start(f32[48,384]{1,0:T(8,128)} %get-tuple-element.35) | copy-start | bytes 221188

commit v3 on v2

v3 whole, which is shorter than its diff:
```python
import functools

import jax
import jax.numpy as jnp
from jax import lax
from jax.experimental import pallas as pl
from jax.experimental.pallas import tpu as pltpu
from jax.sharding import PartitionSpec as P

DMAX = 32
NZ = 8
MESH = pl.DeviceIdType.MESH
BF = jnp.bfloat16
F32 = jnp.float32


def remote(src, dst, send, recv, device):
    return pltpu.make_async_remote_copy(
        src_ref=src, dst_ref=dst, send_sem=send, recv_sem=recv, device_id=device, device_id_type=MESH
    )


def greet(devices):
    barrier = pltpu.get_barrier_semaphore()
    for device in devices:
        pl.semaphore_signal(barrier, inc=1, device_id=device, device_id_type=MESH)
    pl.semaphore_wait(barrier, len(devices))


def z_neighbours():
    z = lax.axis_index("dp")
    return z, lax.rem(z + 1, NZ), lax.rem(z + NZ - 1, NZ)


def seq_neighbours():
    s, n = lax.axis_index("seq"), lax.axis_size("seq")
    return s, lax.rem(s + 1, n), lax.rem(s + n - 1, n)


def whole(n):
    return [pl.BlockSpec(memory_space=pltpu.VMEM)] * n


LO, HI = slice(0, 64), slice(64, 128)
ROWS, PART, RIM = 1024, 512, 8 * DMAX
HALF = (ROWS + PART) // 2
CUBE = 0.044715
SLOPE = 0.7978845608028654


def activate_slope(value):
    square = value * value
    turn = jnp.tanh(SLOPE * (value + CUBE * value * square))
    return 0.5 * (1.0 + turn) + 0.5 * value * (1.0 - turn * turn) * (SLOPE * (1.0 + 3.0 * CUBE * square))


def greet_later(devices):
    barrier = pltpu.get_barrier_semaphore()
    for device in devices:
        pl.semaphore_signal(barrier, inc=1, device_id=device, device_id_type=MESH)
    return lambda: pl.semaphore_wait(barrier, len(devices))


def chunk(i, size):
    return pl.ds(pl.multiple_of(i * size, size), size)


def natural(odd, main, rest):
    return jnp.where(odd, jnp.concatenate([rest, main], axis=1), jnp.concatenate([main, rest], axis=1))


def put_chunk(held, z, slot, hidden):
    odd = lax.rem(z, 2) == 1
    main = jnp.where(odd, hidden[:, 64:192], hidden[:, 0:128])
    rest = jnp.where(odd, hidden[:, 0:64], hidden[:, 128:192])
    held[z, slot, 0:256, :] = main.astype(BF)
    held[z, slot, 256:384, :] = jnp.concatenate([rest[0:128], rest[128:256]], axis=1).astype(BF)


def ring_gather(slot, send_sem, recv_sem, make, on_chunk, on_step, own=None):
    z, right, left = z_neighbours()
    copies = {}

    def start(way, step, c):
        block = lax.rem(z + (-step if way == 0 else step) + NZ, NZ)
        source = own(c) if step == 0 and own else slot(block, c)
        copy = remote(
            source, slot(block, c), send_sem.at[way, step, c], recv_sem.at[way, step, c], {"dp": right if way == 0 else left}
        )
        copy.start()
        copies[way, step, c] = copy

    for c in range(4):
        make(c)
        for way in (0, 1):
            start(way, 0, c)
        on_chunk(0, z, c)
    for step in (1, 2, 3):
        for c in range(4):
            for way in (0, 1):
                copies[way, step - 1, c].wait_recv()
                if step < 3 or c // 2 == way:
                    start(way, step, c)
            on_chunk(2 * step - 1, lax.rem(z - step + NZ, NZ), c)
            on_chunk(2 * step, lax.rem(z + step, NZ), c)
        on_step(step)
    for c in (0, 2, 1, 3):
        copies[c // 2, 3, c].wait_recv()
        on_chunk(7, lax.rem(z + 4, NZ), c)
    on_step(4)
    for copy in copies.values():
        copy.wait_send()


def pair_order(z):
    own, sign = z // 2, 2 * lax.rem(z, 2) - 1
    return [lax.rem(own + d + 4, 4) for d in (0, sign, -sign, 2)]


def unpack_slot(held, pair, slot, put):
    one, two = 2 * pair, 2 * pair + 1
    low, high = held[one, slot, 256:384, :], held[two, slot, 256:384, :]
    mid = jnp.concatenate(
        [jnp.concatenate([low[:, h], high[:, h]], axis=1) for h in (LO, HI)],
        axis=0,
    )
    for i, value in enumerate((held[one, slot, 0:256, :], mid, held[two, slot, 0:256, :])):
        put(pl.ds(pl.multiple_of(384 * pair + 128 * i, 128), 128), value)


def first_kernel(
    gaps,
    x_ref,
    w_ref,
    w_two_ref,
    fe_ref,
    pre_ref,
    hid_ref,
    out_ref,
    pre_two_ref,
    rows_held,
    pre_rows,
    hid_rows,
    held,
    send_sem,
    recv_sem,
    edge_send,
    edge_recv,
    own_sem,
):
    z, right, left = z_neighbours()
    s, after, before = seq_neighbours()
    n = lax.axis_size("seq")
    odd = lax.rem(z, 2) == 1
    mine = pltpu.make_async_copy(x_ref, rows_held.at[z, pl.ds(DMAX, 128)], own_sem)
    mine.start()
    greet_later([{"dp": right}, {"dp": left}, {"seq": after}, {"seq": before}])()
    rims = {}

    def rows_slot(k, c):
        return rows_held.at[k, pl.ds(DMAX + 32 * c, 32)]

    def own_rows(c):
        return x_ref.at[pl.ds(32 * c, 32)]

    def on_rows(order, block, c):
        for at, side, row, peer in ((3, 0, 0, after), (0, 1, DMAX + 128, before)):
            if c == at:
                copy = remote(
                    own_rows(c) if order == 0 else rows_slot(block, c),
                    rows_held.at[block, pl.ds(row, DMAX)],
                    edge_send.at[0, side, order],
                    edge_recv.at[0, side, order],
                    {"seq": peer},
                )
                copy.start()
                rims[side, order] = copy

    def convolve(order):
        shift = (0, -1, 1, -2, 2, -3, 3, 4)[order]
        block = lax.rem(z + shift + NZ, NZ)
        if order == 0:
            mine.wait()
        for side in (0, 1):
            rims[side, order].wait_recv()
        for drop, row in ((s == 0, 0), (s == n - 1, DMAX + 128)):

            @pl.when(drop)
            def _():
                rows_held[block, row : row + DMAX, :] = jnp.zeros((DMAX, 192 * NZ), BF)

        rows = rows_held[block]
        pre = None
        for tap in range(3):
            term = lax.dot_general(rows, w_ref[tap], (((1,), (1,)), ((), ())), preferred_element_type=F32)
            if tap == 1:
                term = term[DMAX : DMAX + 128]
            else:
                first = DMAX + (tap - 1) * gaps[0]
                term = pltpu.roll(term, lax.rem(192 - first, 192), 0)[0:128]
            pre = term if pre is None else pre + term
        main_at, rest_at = 3 * (z // 2) + 2 * lax.rem(z, 2), 3 * (z // 2) + 1
        main = rows_held[block, DMAX : DMAX + 128, pl.ds(pl.multiple_of(128 * main_at, 128), 128)].astype(F32)
        rest = rows_held[block, DMAX : DMAX + 128, pl.ds(pl.multiple_of(128 * rest_at, 128), 128)].astype(F32)
        own = natural(odd, main, jnp.where(odd, rest[:, HI], rest[:, LO]))
        pre_rows[block] = pre
        hid_rows[block] = own + jax.nn.gelu(pre)

    def on_rows_step(step):
        orders = {1: (0,), 2: (1, 2), 3: (3, 4, 5, 6), 4: (7,)}[step]
        for order in orders:
            convolve(order)

    ring_gather(
        rows_slot, send_sem.at[0], recv_sem.at[0], lambda c: None, on_rows, on_rows_step, own_rows
    )
    for copy in rims.values():
        copy.wait_send()

    def make(c):
        bins = slice(32 * c, 32 * c + 32)
        hidden = jnp.swapaxes(hid_rows[:, bins, :], 0, 1).reshape(256, 192)
        hid_ref[256 * c : 256 * c + 256, :] = hidden.astype(BF)
        put_chunk(held, z, 1 + c, hidden)

    edges = {}

    def on_chunk(order, block, c):
        for at, side, slot, peer in ((3, 0, 0, after), (0, 1, 5, before)):
            if c == at:
                copy = remote(
                    held.at[block, 1 + c],
                    held.at[block, slot],
                    edge_send.at[1, side, order],
                    edge_recv.at[1, side, order],
                    {"seq": peer},
                )
                copy.start()
                edges[side, order] = copy

    pairs = pair_order(z)

    def feed(number, orders):
        pair = pairs[number]
        for order in orders:
            for side in (0, 1):
                edges[side, order].wait_recv()

        @pl.loop(0, 6)
        def _(slot):
            keep = jnp.logical_and(jnp.logical_or(slot > 0, s > 0), jnp.logical_or(slot < 5, s < n - 1))

            def put(lanes, value):
                value = jnp.where(keep, value, jnp.zeros_like(value))
                out_ref[chunk(slot, 32), :, lanes] = value.reshape(32, NZ, 128)

            unpack_slot(held, pair, slot, put)

        lanes = chunk(pair, 384)

        @pl.loop(0, 4)
        def _(i):
            total = None
            for tap in range(3):
                rows = out_ref[pl.ds(DMAX + (tap - 1) * gaps[1] + 32 * i, 32), :, lanes].reshape(256, 384)
                term = lax.dot_general(rows, w_two_ref[tap, :, lanes], (((1,), (1,)), ((), ())), preferred_element_type=F32)
                total = term if total is None else total + term
            at = chunk(i, 256)
            pre_two_ref[at, :] = total if number == 0 else pre_two_ref[at, :] + total

    def to_bins(first, last):
        @pl.loop(first, last)
        def _(i):
            fe_ref[chunk(i, 16)] = jnp.swapaxes(rows_held[:, chunk(i, 16), :], 0, 1)

    def on_step(step):
        if step == 1:
            to_bins(0, 7)

            @pl.loop(0, 4)
            def _(i):
                pre_ref[chunk(i, 256), :] = jnp.swapaxes(pre_rows[:, chunk(i, 32), :], 0, 1).reshape(256, 192)

        elif step == 2:
            feed(0, (0, 1, 2))
            to_bins(7, 12)
        elif step == 3:
            feed(1, (3, 4))
            feed(2, (5, 6))
        elif step == 4:
            feed(3, (7,))

    ring_gather(lambda k, c: held.at[k, 1 + c], send_sem.at[1], recv_sem.at[1], make, on_chunk, on_step)
    for copy in edges.values():
        copy.wait_send()


SMEM = pl.BlockSpec(memory_space=pltpu.SMEM)


def call(kernel, name, collective_id, out_shapes, in_specs, scratch, *operands):
    return pl.pallas_call(
        kernel,
        out_shape=tuple(jax.ShapeDtypeStruct(*o) for o in out_shapes),
        in_specs=in_specs,
        out_specs=tuple(whole(len(out_shapes))),
        scratch_shapes=scratch,
        compiler_params=pltpu.CompilerParams(collective_id=collective_id, has_side_effects=True),
        name=name,
    )(*operands)


DMA = pltpu.SemaphoreType.DMA
PACKED = (ROWS + PART, 128)


def first_layer(gaps, rows, weight, weight_two):
    width = rows.shape[1]
    return call(
        first_kernel,
        "first_layer",
        1,
        [
            ((128 + 2 * DMAX, NZ, width), BF),
            ((ROWS, 192), F32),
            ((ROWS, 192), BF),
            ((128 + 2 * DMAX, NZ, width), BF),
            ((ROWS, 192), F32),
        ],
        [SMEM] + whole(3),
        [
            pltpu.VMEM((NZ, 128 + 2 * DMAX, width), BF),
            pltpu.VMEM((NZ, 128, 192), F32),
            pltpu.VMEM((NZ, 128, 192), F32),
            pltpu.VMEM((NZ, 6, 384, 128), BF),
            DMA((2, 2, 4, 4)),
            DMA((2, 2, 4, 4)),
            DMA((2, 2, 8)),
            DMA((2, 2, 8)),
            DMA,
        ],
        gaps,
        rows,
        weight,
        weight_two,
    )


def seq_place():
    s = lax.axis_index("seq")
    return s // 8, lax.rem(s // 2, 4), lax.rem(s, 2)


def seq_peers():
    y, x, core = seq_place()
    at = lambda y, x, core: (y * 4 + x) * 2 + core
    other = at(y, x, 1 - core)
    along_x = [at(y, lax.rem(x + d, 4), core) for d in (1, 2, 3)]
    along_y = [at(lax.rem(y + d, 4), x, core) for d in (1, 2, 3)]
    return other, along_x, along_y


def merge_stats(stats, merged, got, send_sem, recv_sem, own_sem):
    y, x, core = seq_place()
    other, along_x, along_y = seq_peers()
    stages = ((2, core, [other]), (4, x, along_x), (4, y, along_y))
    for number, (count, place, peers) in enumerate(stages):
        source = stats if number == 0 else merged.at[number - 1]
        copies = []
        for d, peer in enumerate(peers):
            copy = remote(
                source, got.at[number, place], send_sem.at[number, d], recv_sem.at[number, d], {"seq": peer}
            )
            copy.start()
            copies.append(copy)
        mine = pltpu.make_async_copy(source, got.at[number, place], own_sem.at[number])
        mine.start()
        mine.wait()
        for copy in copies:
            copy.wait_recv()
        peak = got[number, 0, 0]
        for i in range(1, count):
            peak = jnp.maximum(peak, got[number, i, 0])
        sums = [jnp.zeros_like(peak) for _ in range(3)]
        for i in range(count):
            sums[0] = sums[0] + got[number, i, 1] * jnp.exp(got[number, i, 0] - peak)
            sums[1] = sums[1] + got[number, i, 2]
            sums[2] = sums[2] + got[number, i, 3]
        for copy in copies:
            copy.wait_send()
        if number < 2:
            merged[number, 0] = peak
            for i in range(3):
                merged[number, i + 1] = sums[i]
    return peak, *sums


def second_kernel(
    pre_ref,
    hid_ref,
    head_ref,
    counts_ref,
    out_ref,
    grad_ref,
    loss_ref,
    held,
    logits,
    targets,
    stats,
    merged,
    got,
    send_sem,
    recv_sem,
    stat_send,
    stat_recv,
    stat_own,
):
    z, right, left = z_neighbours()
    other, along_x, along_y = seq_peers()
    met = greet_later([{"dp": right}, {"dp": left}] + [{"seq": p} for p in [other, *along_x, *along_y]])
    shape = stats.shape[1:]

    def make(c):
        rows = slice(256 * c, 256 * c + 256)
        put_chunk(held, z, c, hid_ref[rows, :].astype(F32) + jax.nn.gelu(pre_ref[rows, :]))
        if c == 0:
            met()

    pairs = pair_order(z)

    def feed(number):
        pair = pairs[number]
        lanes = chunk(pair, 384)

        @pl.loop(0, 4)
        def _(i):
            rows = chunk(i, 256)

            def put(at, value):
                out_ref[rows, at] = value

            unpack_slot(held, pair, i, put)
            value = jnp.dot(out_ref[rows, lanes], head_ref[lanes, :], preferred_element_type=F32).reshape(32, *shape)
            logits[chunk(i, 32)] = value if number == 0 else logits[chunk(i, 32)] + value

    def on_step(step):
        feed(step - 1)
        if step in (1, 2):

            @pl.loop(8 * (step - 1), 8 * step)
            def _(i):
                targets[chunk(i, 8)] = jnp.swapaxes(counts_ref[:, chunk(i, 8), :], 0, 1).astype(F32)

    ring_gather(lambda k, c: held.at[k, c], send_sem, recv_sem, make, lambda *_: None, on_step)

    def forward(i, carry):
        peak, count, cross = carry
        value, target = logits[chunk(i, 16)], targets[chunk(i, 16)]
        return (
            jnp.maximum(peak, jnp.max(value, axis=0)),
            count + jnp.sum(target, axis=0),
            cross + jnp.sum(target * value, axis=0),
        )

    zero = jnp.zeros(shape, F32)
    peak, count, cross = lax.fori_loop(0, 8, forward, (jnp.full(shape, -jnp.inf, F32), zero, zero))
    spread = lax.fori_loop(
        0, 8, lambda i, t: t + jnp.sum(jnp.exp(logits[chunk(i, 16)] - peak[None]), axis=0), zero
    )
    for i, value in enumerate((peak, spread, count, cross)):
        stats[i] = value
    peak, spread, count, cross = merge_stats(stats, merged, got, stat_send, stat_recv, stat_own)
    lse = peak + jnp.log(spread)
    bins = 128 * lax.axis_size("seq")
    loss_ref[...] = (count * lse - cross) / bins

    @pl.loop(0, 8)
    def _(i):
        value = (count[None] * jnp.exp(logits[chunk(i, 16)] - lse[None]) - targets[chunk(i, 16)]) * (1.0 / bins)
        grad_ref[chunk(i, 128), :] = value.reshape(128, shape[1]).astype(BF)


def second_layer(pre_two, hidden_one, head_weight, counts):
    tracks = head_weight.shape[1]
    stat = (4, NZ, tracks)
    return call(
        second_kernel,
        "second_layer",
        2,
        [((ROWS, 192 * NZ), BF), ((ROWS, tracks), BF), ((NZ, tracks), F32)],
        whole(4),
        [
            pltpu.VMEM((NZ, 4, 384, 128), BF),
            pltpu.VMEM((128, NZ, tracks), F32),
            pltpu.VMEM((128, NZ, tracks), F32),
            pltpu.VMEM(stat, F32),
            pltpu.VMEM((2, *stat), F32),
            pltpu.VMEM((3, 4, *stat), F32),
            DMA((2, 4, 4)),
            DMA((2, 4, 4)),
            DMA((3, 3)),
            DMA((3, 3)),
            DMA((3,)),
        ],
        pre_two,
        hidden_one,
        head_weight,
        counts,
    )


def ring_scatter(own, got, sent, send_sem, recv_sem, pair_of, hook):
    z, right, left = z_neighbours()
    piece = lambda h: pl.ds(h * HALF, HALF)
    far = lax.rem(z + 4, NZ) // 2
    pair_of(far)
    copies = {}
    for step in range(4):
        for half in (0, 1):
            for way in (0, 1):
                if step == 0 and half != way:
                    continue
                sign = 1 if way == 0 else -1
                block = lax.rem(z + sign * (4 - step) + NZ, NZ)
                before = copies.get((way, step - 1, half))
                if before is None:
                    source = own.at[block, piece(half)]
                else:
                    before.wait_recv()
                    sent[way, step - 1, piece(half), :] = (
                        got[way, step - 1, piece(half), :].astype(F32) + own[block, piece(half), :].astype(F32)
                    ).astype(BF)
                    source = sent.at[way, step - 1, piece(half)]
                copy = remote(
                    source,
                    got.at[way, step, piece(half)],
                    send_sem.at[way, step, half],
                    recv_sem.at[way, step, half],
                    {"dp": right if way == 0 else left},
                )
                copy.start()
                copies[way, step, half] = copy
        if step == 0:
            for d in (1, 3, 2):
                pair_of(lax.rem(far + d, NZ // 2))
        hook(step)
    for half in (0, 1):
        copies[0, 3, half].wait_recv()
        copies[1, 3, half].wait_recv()
    for copy in copies.values():
        copy.wait_send()


def ring_total(own, got, at, size):
    z = lax.axis_index("dp")
    rows = pl.ds(pl.multiple_of(at, 256), size)
    return own[z, rows, :].astype(F32) + got[0, 3, rows, :].astype(F32) + got[1, 3, rows, :].astype(F32)


def ring_result(own, got, i):
    odd = lax.rem(lax.axis_index("dp"), 2) == 1
    rest = ring_total(own, got, ROWS + 256 * i, 256)
    return [
        (index, natural(odd, ring_total(own, got, 256 * index, 256), rest[:, lanes]))
        for index, lanes in ((i, LO), (i + 2, HI))
    ]


def put_pair(own, pair, i, product):
    one, two = 2 * pair, 2 * pair + 1
    for index, value in zip((i, i + 2), product):
        own[one, chunk(index, 256), :] = value[:, 0:128]
        own[two, chunk(index, 256), :] = value[:, 256:384]
    rows = pl.ds(pl.multiple_of(ROWS + 256 * i, 256), 256)
    low, high = product
    own[one, rows, :] = jnp.concatenate([low[:, 128:192], high[:, 128:192]], axis=1)
    own[two, rows, :] = jnp.concatenate([low[:, 192:256], high[:, 192:256]], axis=1)


class Spread:
    def __init__(self, source, result, first, number, scratch):
        self.source, self.result, self.first, self.number = source, result, first, number
        self.pair, self.both, self.early, self.relayed, self.full, self.mid, self.got_two, self.send, self.recv = scratch
        self.y, self.x, self.core = seq_place()
        self.other, self.along_x, self.along_y = seq_peers()

    def stage(self, which):
        along = self.first if which == 1 else ("y" if self.first == "x" else "x")
        return (self.x, self.along_x) if along == "x" else (self.y, self.along_y)

    def copy(self, source, target, slot, peer):
        made = remote(source, target, self.send.at[self.number, slot], self.recv.at[self.number, slot], {"seq": peer})
        made.start()
        return made

    def begin(self):
        self.exchange = self.copy(self.source(1 - self.core), self.pair, 0, self.other)

    def add_pair(self):
        self.exchange.wait_recv()
        mine = self.source(self.core)

        @pl.loop(0, 16)
        def _(i):
            spot = lax.rem(i, 4) * 4 + i // 4 if self.first == "x" else i
            self.both[spot] = (self.pair[i].astype(F32) + mine[i].astype(F32)).astype(BF)

        place, (right, _, left) = self.stage(1)
        far = lax.rem(place + 2, 4)
        self.one, self.last = lax.rem(place + 1, 4), lax.rem(place + 3, 4)
        self.hop = [
            self.copy(self.both.at[pl.ds(4 * far, 2)], self.early.at[0], 1, right),
            self.copy(self.both.at[pl.ds(4 * far + 2, 2)], self.early.at[1], 2, left),
        ]
        self.near = [
            self.copy(self.both.at[pl.ds(4 * self.one + 2, 2)], self.full.at[0, pl.ds(2, 2)], 3, right),
            self.copy(self.both.at[pl.ds(4 * self.last, 2)], self.full.at[1, pl.ds(0, 2)], 4, left),
        ]

    def relay(self):
        _, (right, _, left) = self.stage(1)
        for way, (block, sub, peer) in enumerate(((self.one, 0, right), (self.last, 2, left))):
            self.hop[way].wait_recv()
            for i in range(2):
                total = self.early[way, i].astype(F32) + self.both[4 * block + sub + i].astype(F32)
                self.relayed[way, i] = total.astype(BF)
            self.near.append(self.copy(self.relayed.at[way], self.full.at[way, pl.ds(sub, 2)], 5 + way, peer))

    def add_first(self):
        for copy in self.near:
            copy.wait_recv()
        place, _ = self.stage(1)

        @pl.loop(0, 4)
        def _(i):
            total = self.both[4 * place + i].astype(F32)
            for way in range(2):
                total = total + self.full[way, i].astype(F32)
            self.mid[i] = total.astype(BF)

        place, peers = self.stage(2)
        self.later = []
        for d, peer in enumerate(peers):
            target = lax.rem(place + d + 1, 4)
            self.later.append(self.copy(self.mid.at[target], self.got_two.at[2 - d], 7 + d, peer))

    def finish(self):
        for copy in self.later:
            copy.wait_recv()
        place, _ = self.stage(2)
        total = self.mid[place].astype(F32)
        for d in range(3):
            total = total + self.got_two[d].astype(F32)
        self.result[...] = total
        for copy in [self.exchange, *self.hop, *self.near, *self.later]:
            copy.wait_send()


SPREAD_REFS = 7


def spread_scratch(rows, width):
    return [
        pltpu.VMEM((16, rows, width), BF),
        pltpu.VMEM((16, rows, width), BF),
        pltpu.VMEM((2, 2, rows, width), BF),
        pltpu.VMEM((2, 2, rows, width), BF),
        pltpu.VMEM((2, 4, rows, width), BF),
        pltpu.VMEM((4, rows, width), BF),
        pltpu.VMEM((3, rows, width), BF),
    ]


def conv_pieces(last_split):
    pieces = [(0, 0, 48, "x"), (1, 0, 48, "y")]
    return pieces + ([(2, 0, 16, "x"), (2, 16, 32, "y")] if last_split else [(2, 0, 48, "x")])


def conv_spreads(grads, result, pieces, refs):
    *refs, send, recv = refs
    made = []
    for number, (tap, row, rows, axis) in enumerate(pieces):
        mine = refs[SPREAD_REFS * number : SPREAD_REFS * (number + 1)]
        made.append(
            Spread(
                lambda core, tap=tap, row=row, rows=rows: grads.at[tap, :, core, pl.ds(row, rows)],
                result.at[tap, pl.ds(row, rows)],
                axis,
                number,
                (*mine, send, recv),
            )
        )
    return made


def conv_spread_scratch(pieces):
    made = [pltpu.VMEM((3, 16, 2, 48, 192), BF)]
    for _, _, rows, _ in pieces:
        made += spread_scratch(rows, 192)
    return made + [DMA((len(pieces), 10)), DMA((len(pieces), 10))]


def ring_scratch():
    return [
        pltpu.VMEM((NZ, *PACKED), BF),
        pltpu.VMEM((2, 4, *PACKED), BF),
        pltpu.VMEM((2, 3, *PACKED), BF),
        DMA((2, 4, 2)),
        DMA((2, 4, 2)),
    ]


def seq_hellos():
    other, along_x, along_y = seq_peers()
    return [other, *along_x, *along_y]


def third_kernel(
    grad_ref,
    head_ref,
    rows_ref,
    pre_ref,
    back_ref,
    up_ref,
    head_out,
    own,
    got,
    sent,
    send_sem,
    recv_sem,
    head_grad,
    *rest,
):
    *scratch, edge_send, edge_recv = rest
    z, right, left = z_neighbours()
    s, after, before = seq_neighbours()
    met = greet_later(
        [{"dp": right}, {"dp": left}, {"seq": after}, {"seq": before}] + [{"seq": p} for p in seq_hellos()]
    )
    started = []

    def pair_of(p):
        @pl.loop(0, 2)
        def _(i):
            product = [
                lax.dot_general(
                    grad_ref[chunk(index, 256), :],
                    head_ref[chunk(p, 384), :],
                    (((1,), (1,)), ((), ())),
                    preferred_element_type=F32,
                ).astype(BF)
                for index in (i, i + 2)
            ]
            put_pair(own, p, i, product)

        if not started:
            met()
            started.append(1)

    spread = Spread(lambda core: head_grad.at[:, core], head_out, "x", 0, scratch)

    def hook(step):
        if step == 0:

            @pl.loop(0, 4)
            def _(c):
                value = lax.dot_general(
                    rows_ref[:, chunk(c, 384)], grad_ref[...], (((0,), (0,)), ((), ())), preferred_element_type=F32
                )
                head_grad[chunk(c, 4)] = value.astype(BF).reshape(4, 2, 48, value.shape[1])

            spread.begin()
        elif step == 1:
            spread.add_pair()
        elif step == 2:
            spread.relay()
        else:
            spread.add_first()

    ring_scatter(own, got, sent, send_sem, recv_sem, pair_of, hook)

    @pl.loop(0, 2)
    def _(i):
        for index, value in ring_result(own, got, i):
            back_ref[chunk(index, 256), :] = value
            up = (value * activate_slope(pre_ref[chunk(index, 256), :])).astype(BF)
            up_ref[pl.ds(DMAX + 32 * index, 32)] = up.reshape(32, NZ, 192)

    edges = []
    for side, (src, dst, peer) in enumerate(((128, 0, after), (DMAX, DMAX + 128, before))):
        copy = remote(
            up_ref.at[pl.ds(src, DMAX)], up_ref.at[pl.ds(dst, DMAX)], edge_send.at[side], edge_recv.at[side], {"seq": peer}
        )
        copy.start()
        edges.append(copy)
    for copy in edges:
        copy.wait_recv()
        copy.wait_send()
    for at, drop in ((0, s == 0), (DMAX + 128, s == lax.axis_size("seq") - 1)):

        @pl.when(drop)
        def _():
            up_ref[at : at + DMAX] = jnp.zeros_like(up_ref[at : at + DMAX])

    spread.finish()


def third_layer(logit_grad, head_weight, head_rows, pre_two):
    tracks = head_weight.shape[1]
    return call(
        third_kernel,
        "third_layer",
        3,
        [((ROWS, 192), F32), ((128 + 2 * DMAX, NZ, 192), BF), ((48, tracks), F32)],
        whole(4),
        ring_scratch()
        + [pltpu.VMEM((16, 2, 48, tracks), BF)]
        + spread_scratch(48, tracks)
        + [DMA((1, 10)), DMA((1, 10)), DMA((2,)), DMA((2,))],
        logit_grad,
        head_weight,
        head_rows,
        pre_two,
    )


def tap_grad(framed, spacing, up, tap, into):
    @pl.loop(0, 4)
    def _(c):
        rows = framed[pl.ds(DMAX + (tap - 1) * spacing, 128), :, chunk(c, 384)].reshape(ROWS, 384)
        value = lax.dot_general(rows, up, (((0,), (0,)), ((), ())), preferred_element_type=F32)
        into[chunk(c, 4)] = value.astype(BF).reshape(4, 2, 48, 192)


def fourth_kernel(
    gaps,
    up_ref,
    w_ref,
    back_ref,
    pre_ref,
    f_ref,
    one_ref,
    two_out,
    own,
    got,
    sent,
    send_sem,
    recv_sem,
    grads,
    *spread_refs,
):
    z, right, left = z_neighbours()
    met = greet_later([{"dp": right}, {"dp": left}] + [{"seq": p} for p in seq_hellos()])
    gap = gaps[1]
    started = []

    def pair_of(p):
        @pl.loop(0, 2)
        def _(i):
            product = []
            for index in (i, i + 2):
                total = None
                for tap in range(3):
                    rows = up_ref[pl.ds(DMAX - (tap - 1) * gap + 32 * index, 32)].reshape(256, 192)
                    term = jnp.dot(rows, w_ref[tap, :, chunk(p, 384)], preferred_element_type=F32)
                    total = term if total is None else total + term
                product.append(total.astype(BF))
            put_pair(own, p, i, product)

        if not started:
            met()
            started.append(1)

    spreads = conv_spreads(grads, two_out, conv_pieces(False), spread_refs)

    def hook(step):
        up = lambda: up_ref[DMAX : DMAX + 128].reshape(ROWS, 192)
        if step == 0:
            tap_grad(f_ref, gap, up(), 0, grads.at[0])
            spreads[0].begin()
        elif step == 1:
            tap_grad(f_ref, gap, up(), 1, grads.at[1])
            spreads[1].begin()
            tap_grad(f_ref, gap, up(), 2, grads.at[2])
            spreads[2].begin()
        elif step == 2:
            for t in range(3):
                spreads[t].add_pair()
        else:
            for spread in spreads:
                spread.relay()

    ring_scatter(own, got, sent, send_sem, recv_sem, pair_of, hook)
    for spread in spreads:
        spread.add_first()

    @pl.loop(0, 2)
    def _(i):
        for index, value in ring_result(own, got, i):
            rows = chunk(index, 256)
            one_ref[rows, :] = ((back_ref[rows, :] + value) * activate_slope(pre_ref[rows, :])).astype(BF)

    for t in range(3):
        spreads[t].finish()


def fourth_layer(gaps, framed_up, weight, back, pre_one, framed_one):
    return call(
        fourth_kernel,
        "fourth_layer",
        4,
        [((ROWS, 192), BF), ((3, 48, 192), F32)],
        [SMEM] + whole(5),
        ring_scratch() + conv_spread_scratch(conv_pieces(False)),
        gaps,
        framed_up,
        weight,
        back,
        pre_one,
        framed_one,
    )


def fifth_kernel(gaps, fe_ref, up_ref, one_out, grads, *spread_refs):
    met = greet_later([{"seq": p} for p in seq_hellos()])
    pieces = conv_pieces(True)
    spreads = conv_spreads(grads, one_out, pieces, spread_refs)
    for tap in range(3):
        tap_grad(fe_ref, gaps[0], up_ref[...], tap, grads.at[tap])
        if tap == 0:
            met()
        for piece, spread in zip(pieces, spreads):
            if piece[0] == tap:
                spread.begin()
        if tap == 2:
            spreads[0].add_pair()
    for spread in spreads[1:]:
        spread.add_pair()
    for act in ("relay", "add_first", "finish"):
        for spread in spreads:
            getattr(spread, act)()


def fifth_layer(gaps, framed_in, up_one):
    return call(
        fifth_kernel,
        "fifth_layer",
        5,
        [((3, 48, 192), F32)],
        [SMEM] + whole(2),
        conv_spread_scratch(conv_pieces(True)),
        gaps,
        framed_in,
        up_one,
    )[0]


def on_device(embeddings, conv_one, conv_two, head_weight, counts, dilation):
    framed_in, pre_one, hidden_one, framed_one, pre_two = first_layer(dilation, embeddings[0], conv_one, conv_two)
    head_rows, logit_grad, track_loss = second_layer(pre_two, hidden_one, head_weight, counts)
    grad_two_out, framed_up, grad_head = third_layer(logit_grad, head_weight, head_rows, pre_two)
    up_one, grad_two = fourth_layer(dilation, framed_up, conv_two, grad_two_out, pre_one, framed_one)
    grad_one = fifth_layer(dilation, framed_in, up_one)
    return (track_loss, grad_head, grad_one, grad_two)


def solution(mesh):
    placed = (
        P("dp", "seq", None),
        P(None, "dp", None),
        P(None, "dp", None),
        P(None, "dp"),
        P(None, "seq", "dp"),
        P(),
    )
    return jax.shard_map(
        on_device,
        mesh=mesh,
        in_specs=placed,
        out_specs=(P(None, "dp"), P("seq", "dp"), P(None, "seq", "dp"), P(None, "seq", "dp")),
        check_vma=False,
    )
```

time: 284 us -> 263 us (0.926)
  local copies, waits for them, and re-layouts: 13.2 us -> 3.49 us
  Pallas kernels: 264 us -> 259 us
  other arithmetic: 4.78 us -> 0 us
    pallas_call x1 -> x0, Pallas kernels: 44.5 us -> none  [rows_gather(): pl.pallas_call(rows_gather_kernel, out_shape=jax.ShapeDtypeStruct((NZ, le...]
    pallas_call x5, Pallas kernels: 220 us -> 259 us  [call(): pl.pallas_call(kernel, out_shape=tuple((jax.ShapeDtypeStruct(*o) for o in...]
    pallas_call x1 -> x0, local copies, waits for them, and re-layouts: 7.05 us -> none  [rows_gather(): pl.pallas_call(rows_gather_kernel, out_shape=jax.ShapeDtypeStruct((NZ, le...]
    select_n x3 -> x0, other arithmetic: 4.78 us -> none  [the longest x2 2.45 us: on_device(): jnp.where(odd, jnp.concatenate([g[..., 128:], g[..., :128]], axis=-1), g)]
    slice x12 -> x0, local copies, waits for them, and re-layouts: 3.03 us -> none  [the longest x4 0.9 us: on_device(): w[:, 64:]]
where the time goes in v3:
time: 263 us
  Pallas kernels  259 us (98%)
  local copies, waits for them, and re-layouts  3.49 us (1%)
    pallas_call x5, Pallas kernels, call(): pl.pallas_call(kernel, out_shape=tuple((jax.ShapeDtypeStruct(*o) for o in...  259 us

profile of v3, /device:TPU:2, one launch (start us, length us, event | category | flops | bytes accessed | tf_op | source)
XLA Modules:
  0.0 262.9 jit_solution(17989501451384670521)
XLA Ops:
  0.6 90.1 %first_layer.1 = (bf16[192,8,1536]{2,1,0:T(8,128)(2,1)}, f32[1024,192]{1,0:T(8,128)}, bf16[1024,192]{1,0:T(8,128)(2,1)}, bf16[192,8,1536]{2,1,0:T(8,128)(2,1)}, f32[1024,192]{1,0:T(8,128)}) custom-call(s32[2]{0:T(128)} %gaps.5, bf16[128,1536]{1,0:T(8,128)(2,1)} %bitcast.1, bf16[3,192,1536]{2,1,0:T(8,128)(2,1)} %w_ref.2, bf16[3,192,1536]{2,1,0:T(8,128)(2,1)} %w_ref.3), custom_call_target="tpu_custom_call" | custom-call | tf_op jit(solution)/shard_map/first_layer/pallas_call | solution.py:302
  90.8 55.6 %second_layer.1 = (bf16[1024,1536]{1,0:T(8,128)(2,1)}, bf16[1024,384]{1,0:T(8,128)(2,1)}, f32[8,384]{1,0:T(8,128)}) custom-call(f32[1024,192]{1,0:T(8,128)} %get-tuple-element.17.pre_ref, bf16[1024,192]{1,0:T(8,128)(2,1)} %get-tuple-element.18.hid_ref, bf16[1536,384]{1,0:T(8,128)(2,1)} %head_ref.3, s32[8,128,384]{2,1,0:T(8,128)} %counts_ref.1), custom_call_target="tpu_custom_call" | custom-call | tf_op jit(solution)/shard_map/second_layer/pallas_call | solution.py:302
  146.4 43.2 %third_layer.1 = (f32[1024,192]{1,0:T(8,128)}, bf16[192,8,192]{2,1,0:T(8,128)(2,1)}, f32[48,384]{1,0:T(8,128)}) custom-call(bf16[1024,384]{1,0:T(8,128)(2,1)} %get-tuple-element.20.grad_ref, bf16[1536,384]{1,0:T(8,128)(2,1)} %head_ref.3, bf16[1024,1536]{1,0:T(8,128)(2,1)} %get-tuple-element.21.rows_ref, f32[1024,192]{1,0:T(8,128)} %get-tuple-element.17.pre_ref), custom_call_target="tpu_custom_call" | custom-call | tf_op jit(solution)/shard_map/third_layer/pallas_call | solution.py:302
  189.6 47.3 %fourth_layer.1 = (bf16[1024,192]{1,0:T(8,128)(2,1)}, f32[3,48,192]{2,1,0:T(8,128)}) custom-call(s32[2]{0:T(128)} %gaps.5, bf16[192,8,192]{2,1,0:T(8,128)(2,1)} %get-tuple-element.24.up_ref, bf16[3,192,1536]{2,1,0:T(8,128)(2,1)} %w_ref.3, f32[1024,192]{1,0:T(8,128)} %get-tuple-element.25.back_ref, f32[1024,192]{1,0:T(8,128)} %get-tuple-element.26.pre_ref, ...), custom_call_target="tpu_custom_call" | custom-call | tf_op jit(solution)/shard_map/fourth_layer/pallas_call | solution.py:302
  236.9 0.0 copy-start.2
  236.9 0.0 copy-start.1
  237.0 0.0 copy-start
  237.0 22.4 %fifth_layer.1 = f32[3,48,192]{2,1,0:T(8,128)} custom-call(s32[2]{0:T(128)} %gaps.5, bf16[192,8,1536]{2,1,0:T(8,128)(2,1)} %get-tuple-element.23.fe_ref, bf16[1024,192]{1,0:T(8,128)(2,1)} %get-tuple-element.28.up_ref), custom_call_target="tpu_custom_call" | custom-call | tf_op jit(solution)/shard_map/fifth_layer/pallas_call | solution.py:302
  259.4 0.0 copy-done.2
  259.4 0.6 copy.14
  260.0 0.0 copy-done.1
  260.0 0.6 copy.15
  260.6 1.6 copy.16
  262.2 0.0 copy-done
  262.2 0.7 copy.17
Async XLA Ops:
  236.9 22.4 %copy-start.2 = (f32[8,384]{1,0:T(8,128)S(1)}, f32[8,384]{1,0:T(8,128)}, u32[]{:S(2)}) copy-start(f32[8,384]{1,0:T(8,128)} %get-tuple-element.34) | copy-start | bytes 36868
  236.9 23.1 %copy-start.1 = (f32[48,384]{1,0:T(8,128)S(1)}, f32[48,384]{1,0:T(8,128)}, u32[]{:S(2)}) copy-start(f32[48,384]{1,0:T(8,128)} %get-tuple-element.35) | copy-start | bytes 221188
  237.0 25.3 %copy-start = (f32[3,48,192]{2,1,0:T(8,128)S(1)}, f32[3,48,192]{2,1,0:T(8,128)}, u32[]{:S(2)}) copy-start(f32[3,48,192]{2,1,0:T(8,128)} %get-tuple-element.37) | copy-start | bytes 331780
